TPU v7x, 256 devices: a whole 4x4x8 slice. The times are simulated.
256 devices in a mesh: scen: 8 (over x, z_lo), grid: 32 (over z_hi, y, core).
Axes of the slice: x: 4, y: 4, z: 8 (z_hi: 4, z_lo: 2; z = z_hi * 2 + z_lo), core: 2. Of those that a mesh axis runs over, the one named last changes fastest.
Arguments:
- value_next: float32 [512, 64, 1024], P('grid', 'scen'), may hold values from -8 to 8
- scenario_ids: int32 [8], P('scen'), may hold values from 0 to 11
- inflow_table: int32 [12, 3], replicated, may hold values from 0 to 8, as said below
- release_shifts: int32 [16, 3], replicated, may hold values from 0 to 8, as said below
- price: float32 [3], replicated, may hold values from 0.5 to 4
Outputs:
- value_now: float32 [512, 64, 1024], P('grid', 'scen')
Inputs may be any that keep to these rules, and one draw needn't show every extreme that they name: `inflow_table`: inflows lie in 0 to 8; each draw holds a 0 and an 8. `release_shifts`: releases lie in 0 to 8; one decision releases 8 from every reservoir and one releases nothing.
All inputs are finite; a program needn't handle non-finite values.
Results may differ from a plain program's by a relative error of at most 0.0003.
Values sent between devices are 32-bit elements; how exact they have to be, the bound alone decides.
A program may use at most 128 MiB of HBM per device.

v0:
```python
import jax
import jax.numpy as jnp
from jax import lax
from jax.sharding import Mesh
from jax.sharding import PartitionSpec as P

H = 8
RELEASES = 16
GRID = ("grid_0", "grid_1", "grid_2")
SCEN = ("scen_0", "scen_1")
SCEN_GRID = ("scen_0", "scen_1", "grid_0", "grid_1", "grid_2")


softness = 0.5


def gather_axes(value, axes, dim):
    out = value
    for number in range(len(axes) - 1, -1, -1):
        out = lax.all_gather(out, axes[number], axis=dim, tiled=True)
    return out


def with_halo(cells, sides, width):
    for axis, dim in sides:
        count = lax.axis_size(axis)
        ends = count - 1
        head = lax.slice_in_dim(cells, 0, width, axis=dim)
        tail = lax.slice_in_dim(cells, cells.shape[dim] - width, cells.shape[dim], axis=dim)
        cells = jnp.concatenate(
            [
                lax.ppermute(tail, axis, [(i, (i + 1) % count) for i in range(ends)]),
                cells,
                lax.ppermute(head, axis, [((i + 1) % count, i) for i in range(ends)]),
            ],
            axis=dim,
        )
    return cells


def in_blocks(value, dim, size):
    before, after = (value.shape[:dim], value.shape[dim + 1 :])
    return jnp.moveaxis(value.reshape(*before, size, -1, *after), dim, 0)


def summed_on_arrival(value, axis, dim):
    blocks = in_blocks(value, dim, lax.axis_size(axis))
    arrived = lax.all_to_all(blocks, axis, split_axis=0, concat_axis=0, tiled=True)
    return arrived.sum(axis=0)


def one_axis_at_a_time(value, axes):
    for axis in axes:
        value = lax.psum(value, axis)
    return value


def on_device(value_next, scenario_ids, inflow_table, release_shifts, price):
    row_count = value_next.shape[0]
    share_depth = value_next.shape[1]
    width_count = value_next.shape[2]
    grid_count = lax.axis_size(GRID)
    scen_count = lax.axis_size(SCEN)
    total_rows = row_count * grid_count
    total_depth = share_depth * scen_count
    row_start = lax.axis_index(GRID) * row_count
    spread = gather_axes(value_next, SCEN, 1)
    depth_start = jnp.zeros((), jnp.int32)
    spread = with_halo(spread, ((GRID, 0),), H)
    global_row = row_start - H + jnp.arange(row_count + 2 * H, dtype=jnp.int32)
    local_row = jnp.clip(global_row, 0, total_rows - 1) - (row_start - H)
    global_depth = depth_start - 2 * H + jnp.arange(total_depth + 4 * H, dtype=jnp.int32)
    local_depth = jnp.clip(global_depth, 0, total_depth - 1)
    windowed = jnp.take(jnp.take(spread, local_row, axis=0), local_depth, axis=1)
    wide_pad = 2 * H
    extended = jnp.pad(windowed, ((0, 0), (0, 0), (wide_pad, wide_pad)), mode="edge")
    height_first = (
        (row_start + jnp.arange(row_count, dtype=jnp.int32) + 1).astype(jnp.float32)
        / float(total_rows)
    ).reshape(row_count, 1, 1)
    height_third = (
        (jnp.arange(total_depth, dtype=jnp.int32) + 1).astype(jnp.float32) / float(total_depth)
    ).reshape(1, total_depth, 1)
    height_second = (
        (jnp.arange(width_count) + 1).astype(jnp.float32) / float(width_count)
    ).reshape(1, 1, width_count)
    one_hot = (
        scenario_ids[:, None] == jnp.arange(inflow_table.shape[0], dtype=jnp.int32)[None, :]
    ).astype(jnp.int32)
    inflows = jnp.sum(one_hot[:, :, None] * inflow_table[None, :, :], axis=1)

    def add_release(release_index, running):
        release = release_shifts[release_index]
        amount = release.astype(jnp.float32)
        benefit = (
            price[0] * amount[0] * height_first
            + price[1] * amount[1] * height_second
            + price[2] * amount[2] * height_third
        ) / float(H)

        def one_scenario(inflow):
            first_index = H + inflow[0] - release[0]
            third_index = wide_pad + inflow[2] + release[1] - release[2]
            second_index = wide_pad + inflow[1] + release[0] - release[1]
            return lax.dynamic_slice(
                extended,
                (first_index, third_index, second_index),
                (row_count, total_depth, width_count),
            )

        landed = jax.vmap(one_scenario)(inflows)
        return running + jnp.exp(-(landed - benefit[None]) / softness)

    start_sums = jnp.zeros((inflows.shape[0], row_count, total_depth, width_count), jnp.float32)
    running = lax.fori_loop(0, RELEASES, add_release, start_sums)
    partial_total = jnp.sum(-softness * jnp.log(running), axis=0)
    scenario_count = float(scenario_ids.shape[0] * scen_count)
    owned = summed_on_arrival(partial_total, SCEN, 1)
    average = owned / scenario_count
    cells = float(total_rows * total_depth * width_count)
    level_sum = one_axis_at_a_time(jnp.sum(average), SCEN_GRID)
    return average - level_sum / cells


def solution(mesh):
    torus = Mesh(
        mesh.devices.reshape(4, 2, 4, 4, 2), ("scen_0", "scen_1", "grid_0", "grid_1", "grid_2")
    )
    in_specs = (P(GRID, SCEN, None), P(SCEN), P(), P(), P())
    out_specs = P(GRID, SCEN, None)
    return jax.shard_map(
        on_device, mesh=torus, in_specs=in_specs, out_specs=out_specs, check_vma=False
    )
```

profile of v0, /device:TPU:1, one launch (start us, length us, event | category | flops | bytes accessed | tf_op | source)
XLA Modules:
  0.0 687.7 jit_solution(6352827891274041177)
XLA Ops:
  6.5 0.7 all-gather.3.cloned.1.call-update
  7.3 31.9 %all-gather.3.cloned.1.call-done = f32[16,16,1024]{2,1,0:T(8,128)} async-done(((f32[16,8,1024]{2,1,0:T(8,128)}), f32[16,16,1024]{2,1,0:T(8,128)}) %all-gather.3.cloned.1.call-update) | async-done | bytes 1048592 | tf_op jit(solution)/shard_map/all_gather | solution.py:20
  39.3 52.9 %all-gather.5.cloned.1.call-done = f32[16,64,1024]{2,1,0:T(8,128)} async-done(((f32[16,16,1024]{2,1,0:T(8,128)}), f32[16,64,1024]{2,1,0:T(8,128)}) %all-gather.5.cloned.1.call-update) | async-done | bytes 4194320 | tf_op jit(solution)/shard_map/all_gather | solution.py:20
  92.2 4.0 fusion.18
  96.2 3.8 collective-permute-start
  100.0 1.9 collective-permute-start.1
  102.8 0.6 fusion.19
  105.4 17.9 %collective-permute-done = f32[8,64,1024]{2,1,0:T(8,128)} collective-permute-done((f32[8,64,1024]{2,1,0:T(8,128)}, f32[8,64,1024]{2,1,0:T(8,128)}, u32[]{:S(2)}, u32[]{:S(2)}) %collective-permute-start) | collective-permute-done | bytes 2097184 | tf_op jit(solution)/shard_map/ppermute | solution.py:32
  123.3 4.2 collective-permute-done.1
  127.5 6.0 pad_maximum_fusion
  133.5 7.7 %gather_fusion = f32[32,64,1024]{2,1,0:T(8,128)} fusion(f32[32,64,1024]{2,1,0:T(8,128)} %pad_maximum_fusion, s32[1024]{0:T(1024)S(1)} %pad_clamp_fusion.1), kind=kCustom, calls=%fused_computation | custom fusion | bytes 16777344 | tf_op jit(solution)/shard_map/jit(_take)/gather | solution.py:74
  141.1 4.5 broadcast_select_fusion
  145.6 8.1 %copy.23 = f32[32,64,1024]{2,0,1:T(8,128)} copy(f32[32,64,1024]{2,1,0:T(8,128)S(1)} %broadcast_select_fusion) | data formatting | bytes 16777216 | tf_op jit(solution)/shard_map/jit(_take)/select_n | solution.py:74
  153.7 12.1 %gather_fusion.1 = f32[96,32,1024]{2,1,0:T(8,128)} fusion(f32[32,64,1024]{2,0,1:T(8,128)} %copy.23, s32[1024]{0:T(1024)S(1)} %pad_clamp_fusion), kind=kCustom, calls=%fused_computation.1 | custom fusion | bytes 25166208 | tf_op jit(solution)/shard_map/jit(_take)/gather | solution.py:74
  165.8 12.2 %select_bitcast_fusion = f32[32,96,1024]{2,0,1:T(8,128)} fusion(f32[96,32,1024]{2,1,0:T(8,128)} %gather_fusion.1, pred[96]{0:T(512)(128)(4,1)S(1)} %compare_and_fusion.1), kind=kLoop, calls=%fused_computation.16 | loop fusion | flops 3145728 | bytes 25165920 | tf_op jit(solution)/shard_map/jit(_take)/select_n | solution.py:74
  178.0 2.5 fusion.17
  180.5 0.6 copy.30
  181.1 0.6 copy.31
  182.7 17.0 %concatenate.17 = f32[32,96,1056]{2,0,1:T(8,128)} concatenate(f32[32,96,16]{2,0,1:T(8,128)S(1)} %reshape.240, f32[32,96,1024]{2,0,1:T(8,128)} %select_bitcast_fusion, f32[32,96,16]{2,0,1:T(8,128)S(1)} %reshape.241), dimensions={2} | concatenate | bytes 25952256 | tf_op jit(solution)/shard_map/jit(_pad)/concatenate | solution.py:76
  199.7 377.9 %while.17 = (s32[]{:T(128)}, f32[1,16,64,1024]{3,2,1,0:T(8,128)}, s32[16,3]{0,1:T(4,128)S(1)}, s32[1]{0:T(128)}, s32[1]{0:T(128)}, /*index=5*/s32[1]{0:T(128)}, ...) while((s32[]{:T(128)}, f32[1,16,64,1024]{3,2,1,0:T(8,128)}, ...), condition=%wide.region_2.3_spmd.clone, body=%wide.region_1.2_spmd.clone.sunk | while | flops 7359770 | bytes 21111964 | solution.py:115
  203.4 6.1 dynamic-slice.5
  210.2 0.6 fusion.27
  214.6 7.5 %fusion.29 = f32[1,16,64,1024]{3,2,1,0:T(8,128)} fusion(f32[16,64,1024]{2,0,1:T(8,128)} %dynamic-slice.5, f32[1,16,64,1024]{3,2,1,0:T(8,128)} %get-tuple-element.444, f32[64]{0:T(128)S(1)} %multiply_bitcast_fusion.5, f32[16,1024]{1,0:T(8,128)S(1)} %broadcast_add_fusion.2, pred[]{:T(512)S(6)} %compare.4), kind=kLoop, calls=%fused_computation.10.clone.1 | loop fusion | flops 7340032 | bytes 12648705 | tf_op jit(solution)/shard_map/while/body/eval_jaxpr/add | solution.py:112
  225.8 6.1 dynamic-slice.5
  232.6 0.6 fusion.27
  237.1 8.8 %fusion.29 = f32[1,16,64,1024]{3,2,1,0:T(8,128)} fusion(f32[16,64,1024]{2,0,1:T(8,128)} %dynamic-slice.5, f32[1,16,64,1024]{3,2,1,0:T(8,128)} %get-tuple-element.444, f32[64]{0:T(128)S(1)} %multiply_bitcast_fusion.5, f32[16,1024]{1,0:T(8,128)S(1)} %broadcast_add_fusion.2, pred[]{:T(512)S(6)} %compare.4), kind=kLoop, calls=%fused_computation.10.clone.1 | loop fusion | flops 7340032 | bytes 12648705 | tf_op jit(solution)/shard_map/while/body/eval_jaxpr/add | solution.py:112
  249.5 6.1 dynamic-slice.5
  260.7 8.8 %fusion.29 = f32[1,16,64,1024]{3,2,1,0:T(8,128)} fusion(f32[16,64,1024]{2,0,1:T(8,128)} %dynamic-slice.5, f32[1,16,64,1024]{3,2,1,0:T(8,128)} %get-tuple-element.444, f32[64]{0:T(128)S(1)} %multiply_bitcast_fusion.5, f32[16,1024]{1,0:T(8,128)S(1)} %broadcast_add_fusion.2, pred[]{:T(512)S(6)} %compare.4), kind=kLoop, calls=%fused_computation.10.clone.1 | loop fusion | flops 7340032 | bytes 12648705 | tf_op jit(solution)/shard_map/while/body/eval_jaxpr/add | solution.py:112
  273.2 6.1 dynamic-slice.5
  284.4 8.8 %fusion.29 = f32[1,16,64,1024]{3,2,1,0:T(8,128)} fusion(f32[16,64,1024]{2,0,1:T(8,128)} %dynamic-slice.5, f32[1,16,64,1024]{3,2,1,0:T(8,128)} %get-tuple-element.444, f32[64]{0:T(128)S(1)} %multiply_bitcast_fusion.5, f32[16,1024]{1,0:T(8,128)S(1)} %broadcast_add_fusion.2, pred[]{:T(512)S(6)} %compare.4), kind=kLoop, calls=%fused_computation.10.clone.1 | loop fusion | flops 7340032 | bytes 12648705 | tf_op jit(solution)/shard_map/while/body/eval_jaxpr/add | solution.py:112
  296.9 6.1 dynamic-slice.5
  308.1 8.8 %fusion.29 = f32[1,16,64,1024]{3,2,1,0:T(8,128)} fusion(f32[16,64,1024]{2,0,1:T(8,128)} %dynamic-slice.5, f32[1,16,64,1024]{3,2,1,0:T(8,128)} %get-tuple-element.444, f32[64]{0:T(128)S(1)} %multiply_bitcast_fusion.5, f32[16,1024]{1,0:T(8,128)S(1)} %broadcast_add_fusion.2, pred[]{:T(512)S(6)} %compare.4), kind=kLoop, calls=%fused_computation.10.clone.1 | loop fusion | flops 7340032 | bytes 12648705 | tf_op jit(solution)/shard_map/while/body/eval_jaxpr/add | solution.py:112
  320.6 6.1 dynamic-slice.5
  331.8 8.8 %fusion.29 = f32[1,16,64,1024]{3,2,1,0:T(8,128)} fusion(f32[16,64,1024]{2,0,1:T(8,128)} %dynamic-slice.5, f32[1,16,64,1024]{3,2,1,0:T(8,128)} %get-tuple-element.444, f32[64]{0:T(128)S(1)} %multiply_bitcast_fusion.5, f32[16,1024]{1,0:T(8,128)S(1)} %broadcast_add_fusion.2, pred[]{:T(512)S(6)} %compare.4), kind=kLoop, calls=%fused_computation.10.clone.1 | loop fusion | flops 7340032 | bytes 12648705 | tf_op jit(solution)/shard_map/while/body/eval_jaxpr/add | solution.py:112
  344.3 6.2 dynamic-slice.5
  355.6 8.8 %fusion.29 = f32[1,16,64,1024]{3,2,1,0:T(8,128)} fusion(f32[16,64,1024]{2,0,1:T(8,128)} %dynamic-slice.5, f32[1,16,64,1024]{3,2,1,0:T(8,128)} %get-tuple-element.444, f32[64]{0:T(128)S(1)} %multiply_bitcast_fusion.5, f32[16,1024]{1,0:T(8,128)S(1)} %broadcast_add_fusion.2, pred[]{:T(512)S(6)} %compare.4), kind=kLoop, calls=%fused_computation.10.clone.1 | loop fusion | flops 7340032 | bytes 12648705 | tf_op jit(solution)/shard_map/while/body/eval_jaxpr/add | solution.py:112
  368.0 6.1 dynamic-slice.5
  379.3 8.8 %fusion.29 = f32[1,16,64,1024]{3,2,1,0:T(8,128)} fusion(f32[16,64,1024]{2,0,1:T(8,128)} %dynamic-slice.5, f32[1,16,64,1024]{3,2,1,0:T(8,128)} %get-tuple-element.444, f32[64]{0:T(128)S(1)} %multiply_bitcast_fusion.5, f32[16,1024]{1,0:T(8,128)S(1)} %broadcast_add_fusion.2, pred[]{:T(512)S(6)} %compare.4), kind=kLoop, calls=%fused_computation.10.clone.1 | loop fusion | flops 7340032 | bytes 12648705 | tf_op jit(solution)/shard_map/while/body/eval_jaxpr/add | solution.py:112
  391.7 6.1 dynamic-slice.5
  402.9 8.8 %fusion.29 = f32[1,16,64,1024]{3,2,1,0:T(8,128)} fusion(f32[16,64,1024]{2,0,1:T(8,128)} %dynamic-slice.5, f32[1,16,64,1024]{3,2,1,0:T(8,128)} %get-tuple-element.444, f32[64]{0:T(128)S(1)} %multiply_bitcast_fusion.5, f32[16,1024]{1,0:T(8,128)S(1)} %broadcast_add_fusion.2, pred[]{:T(512)S(6)} %compare.4), kind=kLoop, calls=%fused_computation.10.clone.1 | loop fusion | flops 7340032 | bytes 12648705 | tf_op jit(solution)/shard_map/while/body/eval_jaxpr/add | solution.py:112
  415.4 6.1 dynamic-slice.5
  426.6 8.8 %fusion.29 = f32[1,16,64,1024]{3,2,1,0:T(8,128)} fusion(f32[16,64,1024]{2,0,1:T(8,128)} %dynamic-slice.5, f32[1,16,64,1024]{3,2,1,0:T(8,128)} %get-tuple-element.444, f32[64]{0:T(128)S(1)} %multiply_bitcast_fusion.5, f32[16,1024]{1,0:T(8,128)S(1)} %broadcast_add_fusion.2, pred[]{:T(512)S(6)} %compare.4), kind=kLoop, calls=%fused_computation.10.clone.1 | loop fusion | flops 7340032 | bytes 12648705 | tf_op jit(solution)/shard_map/while/body/eval_jaxpr/add | solution.py:112
  439.1 6.1 dynamic-slice.5
  450.3 8.8 %fusion.29 = f32[1,16,64,1024]{3,2,1,0:T(8,128)} fusion(f32[16,64,1024]{2,0,1:T(8,128)} %dynamic-slice.5, f32[1,16,64,1024]{3,2,1,0:T(8,128)} %get-tuple-element.444, f32[64]{0:T(128)S(1)} %multiply_bitcast_fusion.5, f32[16,1024]{1,0:T(8,128)S(1)} %broadcast_add_fusion.2, pred[]{:T(512)S(6)} %compare.4), kind=kLoop, calls=%fused_computation.10.clone.1 | loop fusion | flops 7340032 | bytes 12648705 | tf_op jit(solution)/shard_map/while/body/eval_jaxpr/add | solution.py:112
  462.8 6.2 dynamic-slice.5
  474.0 8.8 %fusion.29 = f32[1,16,64,1024]{3,2,1,0:T(8,128)} fusion(f32[16,64,1024]{2,0,1:T(8,128)} %dynamic-slice.5, f32[1,16,64,1024]{3,2,1,0:T(8,128)} %get-tuple-element.444, f32[64]{0:T(128)S(1)} %multiply_bitcast_fusion.5, f32[16,1024]{1,0:T(8,128)S(1)} %broadcast_add_fusion.2, pred[]{:T(512)S(6)} %compare.4), kind=kLoop, calls=%fused_computation.10.clone.1 | loop fusion | flops 7340032 | bytes 12648705 | tf_op jit(solution)/shard_map/while/body/eval_jaxpr/add | solution.py:112
  486.5 6.1 dynamic-slice.5
  497.7 8.8 %fusion.29 = f32[1,16,64,1024]{3,2,1,0:T(8,128)} fusion(f32[16,64,1024]{2,0,1:T(8,128)} %dynamic-slice.5, f32[1,16,64,1024]{3,2,1,0:T(8,128)} %get-tuple-element.444, f32[64]{0:T(128)S(1)} %multiply_bitcast_fusion.5, f32[16,1024]{1,0:T(8,128)S(1)} %broadcast_add_fusion.2, pred[]{:T(512)S(6)} %compare.4), kind=kLoop, calls=%fused_computation.10.clone.1 | loop fusion | flops 7340032 | bytes 12648705 | tf_op jit(solution)/shard_map/while/body/eval_jaxpr/add | solution.py:112
  510.2 6.1 dynamic-slice.5
  521.4 8.8 %fusion.29 = f32[1,16,64,1024]{3,2,1,0:T(8,128)} fusion(f32[16,64,1024]{2,0,1:T(8,128)} %dynamic-slice.5, f32[1,16,64,1024]{3,2,1,0:T(8,128)} %get-tuple-element.444, f32[64]{0:T(128)S(1)} %multiply_bitcast_fusion.5, f32[16,1024]{1,0:T(8,128)S(1)} %broadcast_add_fusion.2, pred[]{:T(512)S(6)} %compare.4), kind=kLoop, calls=%fused_computation.10.clone.1 | loop fusion | flops 7340032 | bytes 12648705 | tf_op jit(solution)/shard_map/while/body/eval_jaxpr/add | solution.py:112
  533.9 6.1 dynamic-slice.5
  545.1 8.8 %fusion.29 = f32[1,16,64,1024]{3,2,1,0:T(8,128)} fusion(f32[16,64,1024]{2,0,1:T(8,128)} %dynamic-slice.5, f32[1,16,64,1024]{3,2,1,0:T(8,128)} %get-tuple-element.444, f32[64]{0:T(128)S(1)} %multiply_bitcast_fusion.5, f32[16,1024]{1,0:T(8,128)S(1)} %broadcast_add_fusion.2, pred[]{:T(512)S(6)} %compare.4), kind=kLoop, calls=%fused_computation.10.clone.1 | loop fusion | flops 7340032 | bytes 12648705 | tf_op jit(solution)/shard_map/while/body/eval_jaxpr/add | solution.py:112
  557.6 6.1 dynamic-slice.5
  568.8 8.8 %fusion.29 = f32[1,16,64,1024]{3,2,1,0:T(8,128)} fusion(f32[16,64,1024]{2,0,1:T(8,128)} %dynamic-slice.5, f32[1,16,64,1024]{3,2,1,0:T(8,128)} %get-tuple-element.444, f32[64]{0:T(128)S(1)} %multiply_bitcast_fusion.5, f32[16,1024]{1,0:T(8,128)S(1)} %broadcast_add_fusion.2, pred[]{:T(512)S(6)} %compare.4), kind=kLoop, calls=%fused_computation.10.clone.1 | loop fusion | flops 7340032 | bytes 12648705 | tf_op jit(solution)/shard_map/while/body/eval_jaxpr/add | solution.py:112
  577.6 2.7 multiply_bitcast_fusion.2
  580.9 32.2 %all_to_all.5 = f32[8,16,8,1024]{3,2,1,0:T(8,128)} all-to-all(f32[8,16,8,1024]{3,2,1,0:T(8,128)S(1)} %copy.29), channel_id=1, replica_groups=mesh['scen_0'=4,'scen_1'=2,'grid_0'=4,'grid_1'=4,'grid_2'=2] {'scen_0','..., dimensions={0} | all-to-all | bytes 8388608 | tf_op jit(solution)/shard_map/all_to_all | solution.py:48
  613.1 2.6 reduce_sum.35
  615.7 0.7 multiply_reduce_fusion
  616.4 7.2 %psum.35 = f32[]{:T(128)} all-reduce(f32[]{:T(128)} %multiply_reduce_fusion), channel_id=1, replica_groups=mesh['scen_0'=4,'scen_1'=2,'grid_0'=4,'grid_1'=4,'grid_2'=2] {'scen_0'}, use_global_device_ids=true, to_apply=%region_5.6 | all-reduce | flops 1 | bytes 8 | tf_op jit(solution)/shard_map/psum | solution.py:54
  623.6 4.4 psum.36
  628.0 13.0 %psum.37 = f32[]{:T(128)} all-reduce(f32[]{:T(128)} %psum.36), channel_id=1, replica_groups=mesh['scen_0'=4,'scen_1'=2,'grid_0'=4,'grid_1'=4,'grid_2'=2] {'grid_0'}, use_global_device_ids=true, to_apply=%region_7.8 | all-reduce | flops 1 | bytes 8 | tf_op jit(solution)/shard_map/psum | solution.py:54
  641.0 32.3 %psum.38 = f32[]{:T(128)} all-reduce(f32[]{:T(128)} %psum.37), channel_id=1, replica_groups=mesh['scen_0'=4,'scen_1'=2,'grid_0'=4,'grid_1'=4,'grid_2'=2] {'grid_1'}, use_global_device_ids=true, to_apply=%region_8.9 | all-reduce | flops 1 | bytes 8 | tf_op jit(solution)/shard_map/psum | solution.py:54
  673.3 6.1 psum.39
  680.0 0.8 multiply_subtract_fusion
  (147 shorter events, 32.0 us)
Async XLA Ops:
  6.5 32.7 %all-gather.3.cloned.1.call-start = ((), (), s32[]{:S(2)}) async-start(), calls=%async_computation.1 | async-start | bytes 1572864 | tf_op jit(solution)/shard_map/all_gather | solution.py:20
  7.3 84.9 %all-gather.5.cloned.1.call-start = ((), (), s32[]{:S(2)}) async-start(), calls=%async_computation.2 | async-start | bytes 5242880 | tf_op jit(solution)/shard_map/all_gather | solution.py:20
  39.2 63.4 %copy-start.2 = (s32[12,3]{0,1:T(4,128)S(1)}, s32[12,3]{0,1:T(4,128)}, u32[]{:S(2)}) copy-start(s32[12,3]{0,1:T(4,128)} %param.9) | copy-start | bytes 436
  96.2 27.1 %collective-permute-start = (f32[8,64,1024]{2,1,0:T(8,128)}, f32[8,64,1024]{2,1,0:T(8,128)}, u32[]{:S(2)}, u32[]{:S(2)}) collective-permute-start(f32[8,64,1024]{2,1,0:T(8,128)} %get-tuple-element.343), channel_id=1, source_target_pairs={{0,1},{1,2},{2,3},{3,4},{4,5},{5,6},{6,7},{7,8},{8,9},{9,10},{10,1... | collective-permute-start | bytes 6291464 | tf_op jit(solution)/shard_map/ppermute | solution.py:32
  100.0 27.5 %collective-permute-start.1 = (f32[8,64,1024]{2,1,0:T(8,128)S(1)}, f32[8,64,1024]{2,1,0:T(8,128)}, u32[]{:S(2)}, u32[]{:S(2)}) collective-permute-start(f32[8,64,1024]{2,1,0:T(8,128)S(1)} %get-tuple-element.344), channel_id=1, source_target_pairs={{1,0},{2,1},{3,2},{4,3},{5,4},{6,5},{7,6},{8,7},{9,8},{10,9},{11,1... | collective-permute-start | bytes 6291464 | tf_op jit(solution)/shard_map/ppermute | solution.py:34
  182.7 17.0 %copy-start = (f32[3]{0:T(128)S(1)}, f32[3]{0:T(128)}, u32[]{:S(2)}) copy-start(f32[3]{0:T(128)} %param.11) | copy-start | bytes 40
  182.7 17.0 %copy-start.1 = (s32[16,3]{0,1:T(4,128)S(1)}, s32[16,3]{0,1:T(4,128)}, u32[]{:S(2)}) copy-start(s32[16,3]{0,1:T(4,128)} %param.10) | copy-start | bytes 580
Sparse Core Ops, SparseCore 0:
  9.1 30.0 all-gather.2
  41.0 51.1 all-gather.4
where the time goes:
time: 691 us; the launch traced here: 688 us
  local copies, waits for them, and re-layouts  182 us (26%)
  other arithmetic  172 us (25%)
  loops' own time  109 us (16%)
  waiting for transfers between devices  108 us (16%)
  blocking collectives  95.1 us (14%)
  between operations  16.7 us (2%)
    add x16, other arithmetic, add_release(): return running + jnp.exp(-(landed - benefit[None]) / softness)  139 us
    another operation x1, loops' own time, on_device(): running = lax.fori_loop(0, RELEASES, add_release, start_sums)  109 us
    while x16, local copies, waits for them, and re-layouts, one_scenario(): lax.dynamic_slice(extended, (first_index, third_index, second_index), (ro...  98.2 us
    all_gather x2, waiting for transfers between devices, gather_axes(): out = lax.all_gather(out, axes[number], axis=dim, tiled=True)  84.8 us
    psum x5, blocking collectives, one_axis_at_a_time(): value = lax.psum(value, axis)  62.9 us
    all_to_all x1, blocking collectives, summed_on_arrival(): lax.all_to_all(blocks, axis, split_axis=0, concat_axis=0, tiled=True)  32.2 us
    ppermute x1, waiting for transfers between devices, with_halo(): lax.ppermute(tail, axis, [(i, (i + 1) % count) for i in range(ends)])  17.9 us
    concatenate x1, local copies, waits for them, and re-layouts, on_device(): jnp.pad(windowed, ((0, 0), (0, 0), (wide_pad, wide_pad)), mode='edge')  17 us
  transfers between devices with their start and end apart: 4, of which 4 were waited for; matrix products, arithmetic and copies ran while one was open for 0% of the time, Pallas kernels for 0%

commit v1 on v0

v1 whole, which is shorter than its diff:
```python
import math

import jax
import jax.numpy as jnp
from jax import lax
from jax.experimental import pallas as pl
from jax.experimental.pallas import tpu as pltpu
from jax.sharding import PartitionSpec as P

H = 8
RELEASES = 16
SCENARIOS = 8
LANES = 128
LOG2E = 1.4426950408889634
MESH = pl.DeviceIdType.MESH


def kernel(
    dims,
    x_ref,
    id_ref,
    inflow_ref,
    release_ref,
    price_ref,
    avg_ref,
    mean_ref,
    raw,
    grown,
    own_id,
    all_ids,
    part_a,
    got_a,
    part_b,
    got_b,
    ids_s,
    base_s,
    amount_s,
    rate_s,
    local_sem,
    id_local_sem,
    send_c,
    recv_c,
    send_a,
    recv_a,
    send_id,
    recv_id,
    send_ma,
    recv_ma,
    send_mb,
    recv_mb,
):
    scen_count, grid_count, rows, depth, width = dims
    tiles = width // LANES
    total_rows = rows * grid_count
    total_depth = depth * scen_count
    span = 4 * depth
    reach = rows + 2 * H
    tile_rows = reach * span
    s = lax.axis_index("scen")
    g = lax.axis_index("grid")

    def scen_peer(step):
        return {"scen": lax.rem(s + step + scen_count, scen_count), "grid": g}

    def grid_peer(step):
        return {"scen": s, "grid": lax.rem(g + step + grid_count, grid_count)}

    own_id[...] = jnp.full((1, LANES), id_ref[0], jnp.int32)
    all_ids[s] = jnp.full((1, LANES), id_ref[0], jnp.int32)

    def lanes(i):
        return pl.ds(pl.multiple_of(i * LANES, LANES), LANES)

    def own_copy(i):
        return pltpu.make_async_copy(
            x_ref.at[:, :, lanes(i)], raw.at[i, 1, pl.ds(H, rows)], local_sem.at[i]
        )

    def scen_copy(i, which):
        step, slot = ((1, 0), (-1, 2), (-2, 3))[which]
        return pltpu.make_async_remote_copy(
            src_ref=x_ref.at[:, :, lanes(i)],
            dst_ref=raw.at[i, slot, pl.ds(H, rows)],
            send_sem=send_c.at[i, which],
            recv_sem=recv_c.at[i, which],
            device_id=scen_peer(step),
            device_id_type=MESH,
        )

    def grid_copy(i, slot, way):
        if way == 0:
            first, landing, step = 0, H + rows, -1
        else:
            first, landing, step = rows - H, 0, 1
        if slot == 1:
            source = x_ref.at[pl.ds(first, H), :, lanes(i)]
        else:
            source = raw.at[i, slot, pl.ds(H + first, H)]
        return pltpu.make_async_remote_copy(
            src_ref=source,
            dst_ref=raw.at[i, slot, pl.ds(landing, H)],
            send_sem=send_a.at[i, slot, way],
            recv_sem=recv_a.at[i, slot, way],
            device_id=grid_peer(step),
            device_id_type=MESH,
        )

    def id_copy(step):
        return pltpu.make_async_remote_copy(
            src_ref=own_id,
            dst_ref=all_ids.at[s],
            send_sem=send_id.at[step - 1],
            recv_sem=recv_id.at[step - 1],
            device_id=scen_peer(step),
            device_id_type=MESH,
        )

    def mean_a_copy(step):
        return pltpu.make_async_remote_copy(
            src_ref=part_a,
            dst_ref=got_a.at[step - 1],
            send_sem=send_ma.at[step - 1],
            recv_sem=recv_ma.at[step - 1],
            device_id=scen_peer(step),
            device_id_type=MESH,
        )

    def mean_b_copy(step):
        return pltpu.make_async_remote_copy(
            src_ref=part_b,
            dst_ref=got_b.at[step - 1],
            send_sem=send_mb.at[step - 1],
            recv_sem=recv_mb.at[step - 1],
            device_id=grid_peer(step),
            device_id_type=MESH,
        )

    def loop(start, stop, body):
        def step(i, carry):
            body(i)
            return carry

        lax.fori_loop(start, stop, step, 0)

    barrier = pltpu.get_barrier_semaphore()
    loop(
        1,
        scen_count,
        lambda k: pl.semaphore_signal(barrier, inc=1, device_id=scen_peer(k), device_id_type=MESH),
    )
    loop(
        1,
        grid_count,
        lambda k: pl.semaphore_signal(barrier, inc=1, device_id=grid_peer(k), device_id_type=MESH),
    )
    loop(0, tiles, lambda i: own_copy(i).start())
    pl.semaphore_wait(barrier, scen_count + grid_count - 2)

    loop(1, scen_count, lambda k: id_copy(k).start())

    def start_all(i):
        for which in (0, 1, 2):
            scen_copy(i, which).start()
        for way in (0, 1):
            grid_copy(i, 1, way).start()

    loop(0, tiles, start_all)

    scale = -LOG2E / 4.0

    def rates(r):
        rate_s[0, r] = (price_ref[0] * scale / total_rows) * (H - release_ref[r, 0]).astype(jnp.float32)
        rate_s[1, r] = (price_ref[1] * scale / width) * (H - release_ref[r, 1]).astype(jnp.float32)
        rate_s[2, r] = (price_ref[2] * scale / total_depth) * (H - release_ref[r, 2]).astype(jnp.float32)

    loop(0, RELEASES, rates)

    loop(1, scen_count, lambda k: id_copy(k).wait_recv())
    to_scalar = pltpu.make_async_copy(all_ids, ids_s, id_local_sem)
    to_scalar.start()
    to_scalar.wait()

    def shifts(w):
        row = ids_s[w, 0, 0]
        i1 = inflow_ref[row, 0]
        i2 = inflow_ref[row, 1]
        i3 = inflow_ref[row, 2]

        def one(r):
            u1 = release_ref[r, 0]
            u2 = release_ref[r, 1]
            u3 = release_ref[r, 2]
            along = i2 + u1 - u2
            back = jnp.where(along < 0, 1, 0)
            base_s[w, r] = (1 - back) * tile_rows + (H + i1 - u1) * span + (depth + i3 + u2 - u3)
            amount_s[w, r] = along + back * LANES

        loop(0, RELEASES, one)

    loop(0, scen_count, shifts)

    lane = lax.broadcasted_iota(jnp.int32, (depth, LANES), 1)
    level_c = (lax.broadcasted_iota(jnp.int32, (depth, LANES), 0) + s * depth + 1).astype(jnp.float32)
    level_b = (lane + 1).astype(jnp.float32)
    lowest = jnp.where(g == 0, H, 0)
    highest = jnp.where(g == grid_count - 1, H + rows - 1, reach - 1)
    at_first = s == 0
    at_last = s == scen_count - 1
    near_last = s >= scen_count - 2

    def grow(v):
        return jnp.exp2(v * (-2.0 * LOG2E))

    def build(i):
        def one_row(a):
            source = jnp.clip(a, lowest, highest)
            v0 = raw[i, 0, source]
            v1 = raw[i, 1, source]
            v2 = raw[i, 2, source]
            v3 = raw[i, 3, source]
            v0 = jnp.where(at_first, jnp.broadcast_to(v1[0:1], v0.shape), v0)
            v2 = jnp.where(at_last, jnp.broadcast_to(v1[depth - 1 : depth], v0.shape), v2)
            v3 = jnp.where(near_last, jnp.broadcast_to(v2[depth - 1 : depth], v0.shape), v3)
            at = (i + 1) * tile_rows + a * span
            for slot, v in enumerate((v0, v1, v2, v3)):
                grown[pl.ds(pl.multiple_of(at + slot * depth, depth), depth), :] = grow(v)

        loop(0, reach, one_row)

    def edge(from_tile, to_tile, column):
        def one(k):
            at = pl.multiple_of(k * depth, depth)
            v = grown[pl.ds(from_tile * tile_rows + at, depth), :]
            grown[pl.ds(to_tile * tile_rows + at, depth), :] = jnp.broadcast_to(
                v[:, column : column + 1], (depth, LANES)
            )

        loop(0, tile_rows // depth, one)

    group = 4

    def compute(j, total):
        level = level_b + (j * LANES).astype(jnp.float32)

        def one_group(q, total):
            first = q * group

            def one_release(r, sums):
                sums = list(sums)
                flat = rate_s[2, r] * level_c + rate_s[1, r] * level
                weights = []
                for k in range(group):
                    row = (g * rows + first + k + 1).astype(jnp.float32)
                    weights.append(jnp.exp2(flat + rate_s[0, r] * row))
                for w in range(SCENARIOS):
                    at = base_s[w, r] + j * tile_rows + first * span
                    amount = amount_s[w, r]
                    mask = lane < amount
                    turn = jnp.bitwise_and(LANES - amount, LANES - 1)
                    for k in range(group):
                        low = grown[pl.ds(at + k * span, depth), :]
                        high = grown[pl.ds(at + k * span + tile_rows, depth), :]
                        landed = pltpu.roll(jnp.where(mask, high, low), turn, 1)
                        sums[w * group + k] = sums[w * group + k] + weights[k] * landed
                return tuple(sums)

            zero = jnp.zeros((depth, LANES), jnp.float32)
            sums = lax.fori_loop(0, RELEASES, one_release, (zero,) * (SCENARIOS * group))
            for k in range(group):
                t = [sums[w * group + k] for w in range(SCENARIOS)]
                logs = jnp.log(t[0] * t[1] * (t[2] * t[3])) + jnp.log(t[4] * t[5] * (t[6] * t[7]))
                row = (g * rows + first + k + 1).astype(jnp.float32)
                top = (
                    (price_ref[2] / total_depth) * level_c
                    + (price_ref[1] / width) * level
                    + (price_ref[0] / total_rows) * row
                )
                value = -top - (0.5 / SCENARIOS) * logs
                avg_ref[first + k, :, lanes(j)] = value
                total = total + value
            return total

        return lax.fori_loop(0, rows // group, one_group, total)

    def finish(i):
        for slot in range(4):
            for way in (0, 1):
                grid_copy(i, slot, way).wait_recv()
        build(i)

    def step(i, total):
        own_copy(i).wait()
        for which, slot in ((0, 0), (1, 2), (2, 3)):
            scen_copy(i, which).wait_recv()
            for way in (0, 1):
                grid_copy(i, slot, way).start()

        @pl.when(i >= 1)
        def _():
            finish(i - 1)

        @pl.when(i == 1)
        def _():
            edge(1, 0, 0)

        return lax.cond(i >= 2, lambda t: compute(i - 2, t), lambda t: t, total)

    total = jnp.zeros((depth, LANES), jnp.float32)
    total = lax.fori_loop(0, tiles, step, total)
    finish(tiles - 1)
    edge(tiles, tiles + 1, LANES - 1)
    total = lax.fori_loop(tiles - 2, tiles, compute, total)

    part_a[...] = jnp.sum(total, axis=0, keepdims=True)
    loop(1, scen_count, lambda k: mean_a_copy(k).start())
    loop(1, scen_count, lambda k: mean_a_copy(k).wait_recv())
    part_b[...] = part_a[...] + jnp.sum(got_a[...], axis=0)
    loop(1, grid_count, lambda k: mean_b_copy(k).start())
    loop(1, grid_count, lambda k: mean_b_copy(k).wait_recv())
    whole = part_b[...] + jnp.sum(got_b[...], axis=0)
    cells = float(total_rows * total_depth * width)
    mean_ref[...] = jnp.broadcast_to(jnp.sum(whole, axis=1, keepdims=True) / cells, (1, LANES))

    loop(1, scen_count, lambda k: id_copy(k).wait_send())
    loop(1, scen_count, lambda k: mean_a_copy(k).wait_send())
    loop(1, grid_count, lambda k: mean_b_copy(k).wait_send())

    def drain(i):
        for which in (0, 1, 2):
            scen_copy(i, which).wait_send()
        for slot in range(4):
            for way in (0, 1):
                grid_copy(i, slot, way).wait_send()

    loop(0, tiles, drain)


def solution(mesh):
    scen_count = mesh.shape["scen"]
    grid_count = mesh.shape["grid"]

    def on_device(value_next, scenario_ids, inflow_table, release_shifts, price):
        rows, depth, width = value_next.shape
        tiles = width // LANES
        dims = (scen_count, grid_count, rows, depth, width)
        reach = rows + 2 * H
        smem = pl.BlockSpec(memory_space=pltpu.SMEM)
        vmem = pl.BlockSpec(memory_space=pltpu.VMEM)
        dma = pltpu.SemaphoreType.DMA
        average, mean = pl.pallas_call(
            lambda *refs: kernel(dims, *refs),
            out_shape=(
                jax.ShapeDtypeStruct((rows, depth, width), jnp.float32),
                jax.ShapeDtypeStruct((1, LANES), jnp.float32),
            ),
            in_specs=[pl.BlockSpec(memory_space=pl.ANY), smem, smem, smem, smem],
            out_specs=(vmem, vmem),
            scratch_shapes=[
                pltpu.VMEM((tiles, 4, reach, depth, LANES), jnp.float32),
                pltpu.VMEM(((tiles + 2) * reach * 4 * depth, LANES), jnp.float32),
                pltpu.VMEM((1, LANES), jnp.int32),
                pltpu.VMEM((scen_count, 1, LANES), jnp.int32),
                pltpu.VMEM((1, LANES), jnp.float32),
                pltpu.VMEM((scen_count - 1, 1, LANES), jnp.float32),
                pltpu.VMEM((1, LANES), jnp.float32),
                pltpu.VMEM((grid_count - 1, 1, LANES), jnp.float32),
                pltpu.SMEM((scen_count, 1, LANES), jnp.int32),
                pltpu.SMEM((SCENARIOS, RELEASES), jnp.int32),
                pltpu.SMEM((SCENARIOS, RELEASES), jnp.int32),
                pltpu.SMEM((3, RELEASES), jnp.float32),
                dma((tiles,)),
                dma,
                dma((tiles, 3)),
                dma((tiles, 3)),
                dma((tiles, 4, 2)),
                dma((tiles, 4, 2)),
                dma((scen_count - 1,)),
                dma((scen_count - 1,)),
                dma((scen_count - 1,)),
                dma((scen_count - 1,)),
                dma((grid_count - 1,)),
                dma((grid_count - 1,)),
            ],
            compiler_params=pltpu.CompilerParams(
                collective_id=0, has_side_effects=True, vmem_limit_bytes=40 * 1024 * 1024
            ),
        )(value_next, scenario_ids, inflow_table, release_shifts, price)
        return average - mean[0, 0]

    return jax.shard_map(
        on_device,
        mesh=mesh,
        in_specs=(P("grid", "scen", None), P("scen"), P(), P(), P()),
        out_specs=P("grid", "scen", None),
        check_vma=False,
    )
```

time: 691 us -> 141 us (0.20)
  local copies, waits for them, and re-layouts: 182 us -> 2.48 us
  other arithmetic: 172 us -> 0.87 us
  Pallas kernels: 0 us -> 137 us
  loops' own time: 109 us -> 0 us
  waiting for transfers between devices: 108 us -> 0 us
  blocking collectives: 95.1 us -> 0 us
  between operations: 16.7 us -> 0.67 us
    add x32 -> x0, other arithmetic: 141 us -> none  [the longest x16 139 us: add_release(): return running + jnp.exp(-(landed - benefit[None]) / softness)]
    pallas_call x0 -> x1, Pallas kernels: none -> 137 us  [on_device(): pl.pallas_call(lambda *refs: kernel(dims, *refs), out_shape=(jax.ShapeDty...]
    another operation x1 -> x0, loops' own time: 109 us -> none  [on_device(): running = lax.fori_loop(0, RELEASES, add_release, start_sums)]
    while x16 -> x0, local copies, waits for them, and re-layouts: 98.2 us -> none  [one_scenario(): lax.dynamic_slice(extended, (first_index, third_index, second_index), (ro...]
    all_gather x2 -> x0, waiting for transfers between devices: 84.8 us -> none  [gather_axes(): out = lax.all_gather(out, axes[number], axis=dim, tiled=True)]
    psum x5 -> x0, blocking collectives: 62.9 us -> none  [one_axis_at_a_time(): value = lax.psum(value, axis)]
    slice x53 -> x0, local copies, waits for them, and re-layouts: 37 us -> none  [the longest x16 9.8 us: add_release(): price[0] * amount[0] * height_first + price[1] * amount[1] * height_second]
    all_to_all x1 -> x0, blocking collectives: 32.2 us -> none  [summed_on_arrival(): lax.all_to_all(blocks, axis, split_axis=0, concat_axis=0, tiled=True)]
  transfers between devices with their start and end apart: 4 -> 0, of which waited for: 4 -> 0; matrix products, arithmetic and copies ran while one was open for 0% -> 0% of each run, Pallas kernels for 0% -> 0%
where the time goes in v1:
time: 141 us
  Pallas kernels  137 us (97%)
  local copies, waits for them, and re-layouts  2.48 us (2%)
    pallas_call x1, Pallas kernels, on_device(): pl.pallas_call(lambda *refs: kernel(dims, *refs), out_shape=(jax.ShapeDty...  137 us

profile of v1, /device:TPU:1, one launch (start us, length us, event | category | flops | bytes accessed | tf_op | source)
XLA Modules:
  0.0 140.7 jit_solution(13028160359031988664)
XLA Ops:
  0.7 0.0 copy-start.2
  0.7 0.8 copy.6.refs_2_
  1.4 0.0 copy-done.2
  1.4 0.0 copy-start.1
  1.4 0.1 copy.7.refs_3_
  1.5 0.6 copy-done.1
  2.1 0.0 copy-start
  2.1 1.0 copy-done
  3.1 136.7 %shard_map.55 = (f32[16,8,1024]{2,1,0:T(8,128)S(1)}, f32[1,128]{1,0:T(1,128)S(1)}) custom-call(f32[16,8,1024]{2,1,0:T(8,128)S(1)} %copy-done, s32[1]{0:T(128)S(6)} %copy.8.refs_1_, s32[12,3]{1,0:T(8,128)S(1)} %copy.6.refs_2_, s32[16,3]{1,0:T(8,128)S(1)} %copy.7.refs_3_, f32[3]{0:T(128)S(1)} %copy-done.1), custom_call_target="tpu_custom_call" | custom-call | tf_op jit(solution)/shard_map/pallas_call | solution.py:350
  139.9 0.9 broadcast_subtract_fusion
Async XLA Ops:
  0.7 0.8 copy-start.2
  1.4 0.7 copy-start.1
  2.1 1.0 copy-start

commit v2 on v1

v2 whole, which is shorter than its diff:
```python
import math

import jax
import jax.numpy as jnp
from jax import lax
from jax.experimental import pallas as pl
from jax.experimental.pallas import tpu as pltpu
from jax.sharding import PartitionSpec as P

H = 8
RELEASES = 16
SCENARIOS = 8
LANES = 128
LOG2E = 1.4426950408889634
MESH = pl.DeviceIdType.MESH
NEAR = 8


def kernel(
    dims,
    x_ref,
    id_hbm,
    inflow_hbm,
    release_hbm,
    price_hbm,
    avg_ref,
    mean_ref,
    raw,
    grown,
    own_id,
    all_ids,
    part_a,
    got_a,
    part_b,
    got_b,
    part_c,
    got_c,
    ids_s,
    id_ref,
    inflow_ref,
    release_ref,
    price_ref,
    base_s,
    amount_s,
    turn_s,
    rate_s,
    local_sem,
    small_sem,
    id_local_sem,
    send_c,
    recv_c,
    send_a,
    recv_a,
    send_id,
    recv_id,
    send_ma,
    recv_ma,
    send_mb,
    recv_mb,
    send_mc,
    recv_mc,
):
    scen_count, grid_count, rows, depth, width = dims
    tiles = width // LANES
    total_rows = rows * grid_count
    total_depth = depth * scen_count
    span = 4 * depth
    reach = rows + 2 * H
    tile_rows = reach * span
    s = lax.axis_index("scen")
    g = lax.axis_index("grid")

    def scen_peer(step):
        return {"scen": lax.rem(s + step + scen_count, scen_count), "grid": g}

    def grid_peer(step):
        return {"scen": s, "grid": lax.rem(g + step + grid_count, grid_count)}

    near = lax.rem(g, NEAR)

    def near_peer(step):
        return {"scen": s, "grid": g - near + lax.rem(near + step, NEAR)}


    def lanes(i):
        return pl.ds(pl.multiple_of(i * LANES, LANES), LANES)

    def own_copy(i):
        return pltpu.make_async_copy(
            x_ref.at[:, :, lanes(i)], raw.at[i, 1, pl.ds(H, rows)], local_sem.at[i]
        )

    def block_copy(i, source, slot, step, use):
        return pltpu.make_async_remote_copy(
            src_ref=x_ref.at[:, :, lanes(i)] if source == 1 else raw.at[i, source, pl.ds(H, rows)],
            dst_ref=raw.at[i, slot, pl.ds(H, rows)],
            send_sem=send_c.at[i, use],
            recv_sem=recv_c.at[i, slot],
            device_id=scen_peer(step),
            device_id_type=MESH,
        )

    def two_back(i):
        return block_copy(i, 1, 3, -2, 0)

    def up(i):
        return block_copy(i, 1, 0, 1, 1)

    def down(i):
        return block_copy(i, 1, 2, -1, 1)

    def relay_up(i):
        return block_copy(i, 2, 0, 2, 2)

    def relay_down(i):
        return block_copy(i, 0, 2, -2, 2)

    def relay_across(i):
        return block_copy(i, 3, 2, 1, 3)

    def landed(i, slot):
        return block_copy(i, 1, slot, -2, 0)

    def grid_copy(i, slot, way):
        if way == 0:
            first, landing, step = 0, H + rows, -1
        else:
            first, landing, step = rows - H, 0, 1
        if slot == 1:
            source = x_ref.at[pl.ds(first, H), :, lanes(i)]
        else:
            source = raw.at[i, slot, pl.ds(H + first, H)]
        return pltpu.make_async_remote_copy(
            src_ref=source,
            dst_ref=raw.at[i, slot, pl.ds(landing, H)],
            send_sem=send_a.at[i, slot, way],
            recv_sem=recv_a.at[i, slot, way],
            device_id=grid_peer(step),
            device_id_type=MESH,
        )

    def halo_copy(i, which, way):
        step, slot = ((1, 0), (-1, 2), (-2, 3))[which]
        landing = H + rows if way == 0 else 0
        return pltpu.make_async_remote_copy(
            src_ref=raw.at[i, 1, pl.ds(landing, H)],
            dst_ref=raw.at[i, slot, pl.ds(landing, H)],
            send_sem=send_a.at[i, slot, 1 - way],
            recv_sem=recv_a.at[i, slot, way],
            device_id=scen_peer(step),
            device_id_type=MESH,
        )

    def id_copy(step):
        return pltpu.make_async_remote_copy(
            src_ref=own_id,
            dst_ref=all_ids.at[s],
            send_sem=send_id.at[step - 1],
            recv_sem=recv_id.at[step - 1],
            device_id=scen_peer(step),
            device_id_type=MESH,
        )

    def mean_a_copy(step):
        return pltpu.make_async_remote_copy(
            src_ref=part_a,
            dst_ref=got_a.at[step - 1],
            send_sem=send_ma.at[step - 1],
            recv_sem=recv_ma.at[step - 1],
            device_id=scen_peer(step),
            device_id_type=MESH,
        )

    def mean_b_copy(step):
        return pltpu.make_async_remote_copy(
            src_ref=part_b,
            dst_ref=got_b.at[step - 1],
            send_sem=send_mb.at[step - 1],
            recv_sem=recv_mb.at[step - 1],
            device_id=near_peer(step),
            device_id_type=MESH,
        )

    def mean_c_copy(step):
        return pltpu.make_async_remote_copy(
            src_ref=part_c,
            dst_ref=got_c.at[step - 1],
            send_sem=send_mc.at[step - 1],
            recv_sem=recv_mc.at[step - 1],
            device_id=grid_peer(step * NEAR),
            device_id_type=MESH,
        )

    def loop(start, stop, body):
        def step(i, carry):
            body(i)
            return carry

        lax.fori_loop(start, stop, step, 0)

    barrier = pltpu.get_barrier_semaphore()

    def greet(peer):
        pl.semaphore_signal(barrier, inc=1, device_id=peer, device_id_type=MESH)

    far_count = grid_count // NEAR
    for step in range(1, scen_count):
        greet(scen_peer(step))
    for step in range(1, NEAR):
        greet(near_peer(step))
    for step in range(1, far_count):
        greet(grid_peer(step * NEAR))
    for step in (-1, 1):
        greet(grid_peer(step))
    small = [
        pltpu.make_async_copy(source, target, small_sem.at[n])
        for n, (source, target) in enumerate(
            ((id_hbm, id_ref), (inflow_hbm, inflow_ref), (release_hbm, release_ref), (price_hbm, price_ref))
        )
    ]
    for copy in small:
        copy.start()
    for i in range(tiles):
        own_copy(i).start()
    for copy in small:
        copy.wait()
    own_id[...] = jnp.full((1, LANES), id_ref[0], jnp.int32)
    all_ids[s] = jnp.full((1, LANES), id_ref[0], jnp.int32)
    pl.semaphore_wait(barrier, scen_count + NEAR + far_count - 1)

    even = lax.rem(s, 2) == 0
    odd = jnp.logical_not(even)
    crosses = (near == 0, near == NEAR - 1)

    def start_all(i):
        for way in (0, 1):
            grid_copy(i, 1, way).start()

        @pl.when(even)
        def _():
            up(i).start()

        @pl.when(odd)
        def _():
            down(i).start()

        two_back(i).start()

    def pass_on(i, slot):
        for way in (0, 1):

            @pl.when(jnp.logical_not(crosses[way]))
            def _():
                grid_copy(i, slot, way).start()

    def by_x(i):
        return lax.rem(i, 4) != 3

    def forward_first(i):
        @pl.when(even)
        def _():
            landed(i, 2).wait_recv()
            relay_up(i).start()
            pass_on(i, 2)

        @pl.when(odd)
        def _():
            landed(i, 0).wait_recv()

            @pl.when(by_x(i))
            def _():
                relay_down(i).start()

            pass_on(i, 0)

        landed(i, 3).wait_recv()

        @pl.when(jnp.logical_and(even, jnp.logical_not(by_x(i))))
        def _():
            relay_across(i).start()

        pass_on(i, 3)
        for way in (0, 1):
            grid_copy(i, 1, way).wait_recv()

            @pl.when(crosses[1 - way])
            def _():
                for which in (0, 1, 2):
                    halo_copy(i, which, way).start()

    def forward_second(i):
        @pl.when(even)
        def _():
            landed(i, 0).wait_recv()
            pass_on(i, 0)

        @pl.when(odd)
        def _():
            landed(i, 2).wait_recv()
            pass_on(i, 2)

    ahead = 3
    for i in range(ahead):
        start_all(i)
    for step in range(1, scen_count):
        id_copy(step).start()
    forward_first(0)

    scale = -LOG2E / 4.0

    def rates(r):
        rate_s[0 * RELEASES + r] = (price_ref[0] * scale / total_rows) * (H - release_ref[0, r]).astype(jnp.float32)
        rate_s[1 * RELEASES + r] = (price_ref[1] * scale / width) * (H - release_ref[1, r]).astype(jnp.float32)
        rate_s[2 * RELEASES + r] = (price_ref[2] * scale / total_depth) * (H - release_ref[2, r]).astype(jnp.float32)

    loop(0, RELEASES, rates)

    for step in range(1, scen_count):
        id_copy(step).wait_recv()
    to_scalar = pltpu.make_async_copy(all_ids, ids_s, id_local_sem)
    to_scalar.start()
    to_scalar.wait()

    def shifts(w):
        row = ids_s[w, 0, 0]
        i1 = inflow_ref[0, row]
        i2 = inflow_ref[1, row]
        i3 = inflow_ref[2, row]

        def one(r):
            u1 = release_ref[0, r]
            u2 = release_ref[1, r]
            u3 = release_ref[2, r]
            along = i2 + u1 - u2
            back = jnp.where(along < 0, 1, 0)
            at = r * SCENARIOS + w
            amount = along + back * LANES
            base_s[at] = (1 - back) * tile_rows + (H + i1 - u1) * span + (depth + i3 + u2 - u3)
            amount_s[at] = amount
            turn_s[at] = jnp.bitwise_and(LANES - amount, LANES - 1)

        loop(0, RELEASES, one)

    loop(0, scen_count, shifts)

    lane = lax.broadcasted_iota(jnp.int32, (depth, LANES), 1)
    level_c = (lax.broadcasted_iota(jnp.int32, (depth, LANES), 0) + s * depth + 1).astype(jnp.float32)
    level_b = (lane + 1).astype(jnp.float32)
    lowest = jnp.where(g == 0, H, 0)
    highest = jnp.where(g == grid_count - 1, H + rows - 1, reach - 1)
    at_first = s == 0
    at_last = s == scen_count - 1
    near_last = s >= scen_count - 2

    def grow(v):
        return jnp.exp2(v * (-2.0 * LOG2E))

    def build(i):
        def some_rows(block):
            for k in range(4):
                a = block * 4 + k
                source = jnp.clip(a, lowest, highest)
                v0 = raw[i, 0, source]
                v1 = raw[i, 1, source]
                v2 = raw[i, 2, source]
                v3 = raw[i, 3, source]
                v0 = jnp.where(at_first, jnp.broadcast_to(v1[0:1], v0.shape), v0)
                v2 = jnp.where(at_last, jnp.broadcast_to(v1[depth - 1 : depth], v0.shape), v2)
                v3 = jnp.where(near_last, jnp.broadcast_to(v2[depth - 1 : depth], v0.shape), v3)
                at = (i + 1) * tile_rows + a * span
                for slot, v in enumerate((v0, v1, v2, v3)):
                    grown[pl.ds(pl.multiple_of(at + slot * depth, depth), depth), :] = grow(v)

        loop(0, reach // 4, some_rows)

    def edge(from_tile, to_tile, column):
        def some(block):
            for k in range(16):
                at = pl.multiple_of((block * 16 + k) * depth, depth)
                v = grown[pl.ds(from_tile * tile_rows + at, depth), :]
                grown[pl.ds(to_tile * tile_rows + at, depth), :] = jnp.broadcast_to(
                    v[:, column : column + 1], (depth, LANES)
                )

        loop(0, tile_rows // depth // 16, some)

    group = 4

    def compute(j, total):
        level = level_b + (j * LANES).astype(jnp.float32)

        def one_group(q, total):
            first = q * group
            offset = j * tile_rows + first * span

            def one_release(r, sums):
                sums = list(sums)
                flat = rate_s[2 * RELEASES + r] * level_c + rate_s[1 * RELEASES + r] * level
                weights = []
                for k in range(group):
                    row = (g * rows + first + k + 1).astype(jnp.float32)
                    weights.append(jnp.exp2(flat + rate_s[0 * RELEASES + r] * row))
                for w in range(SCENARIOS):
                    at = base_s[r * SCENARIOS + w] + offset
                    mask = lane < amount_s[r * SCENARIOS + w]
                    turn = turn_s[r * SCENARIOS + w]
                    for k in range(group):
                        low = grown[pl.ds(at + k * span, depth), :]
                        high = grown[pl.ds(at + k * span + tile_rows, depth), :]
                        landed = pltpu.roll(jnp.where(mask, high, low), turn, 1)
                        sums[w * group + k] = sums[w * group + k] + weights[k] * landed
                return tuple(sums)

            zero = jnp.zeros((depth, LANES), jnp.float32)
            sums = (zero,) * (SCENARIOS * group)
            for r in range(RELEASES):
                sums = one_release(r, sums)
            for k in range(group):
                t = [sums[w * group + k] for w in range(SCENARIOS)]
                logs = jnp.log(t[0] * t[1] * (t[2] * t[3])) + jnp.log(t[4] * t[5] * (t[6] * t[7]))
                row = (g * rows + first + k + 1).astype(jnp.float32)
                top = (
                    (price_ref[2] / total_depth) * level_c
                    + (price_ref[1] / width) * level
                    + (price_ref[0] / total_rows) * row
                )
                value = -top - (0.5 / SCENARIOS) * logs
                avg_ref[first + k, :, lanes(j)] = value
                total = total + value
            return total

        return lax.fori_loop(0, rows // group, one_group, total)

    def finish(i):
        own_copy(i).wait()
        for slot in (0, 2, 3):
            for way in (0, 1):
                grid_copy(i, slot, way).wait_recv()
        build(i)

    def step(i, total):
        @pl.when(i + ahead - 1 < tiles)
        def _():
            start_all(i + ahead - 1)

        @pl.when(i < tiles)
        def _():
            forward_first(i)

        forward_second(i - 1)
        total = lax.cond(i >= 3, lambda t: compute(i - 3, t), lambda t: t, total)
        finish(i - 1)

        @pl.when(i == 1)
        def _():
            edge(1, 0, 0)

        return total

    total = jnp.zeros((depth, LANES), jnp.float32)
    total = lax.fori_loop(1, tiles + 1, step, total)
    edge(tiles, tiles + 1, LANES - 1)
    total = lax.fori_loop(tiles - 2, tiles, compute, total)

    def drain(i):
        two_back(i).wait_send()
        up(i).wait_send()

        @pl.when(jnp.logical_or(even, by_x(i)))
        def _():
            relay_up(i).wait_send()

        @pl.when(jnp.logical_and(even, jnp.logical_not(by_x(i))))
        def _():
            relay_across(i).wait_send()

        for slot in range(4):
            for way in (0, 1):
                grid_copy(i, slot, way).wait_send()

    part_a[...] = jnp.sum(total, axis=0, keepdims=True)
    for step in range(1, scen_count):
        mean_a_copy(step).start()
    for step in range(1, scen_count):
        id_copy(step).wait_send()
    loop(0, tiles, drain)
    for step in range(1, scen_count):
        mean_a_copy(step).wait_recv()
    part_b[...] = part_a[...] + jnp.sum(got_a[...], axis=0)
    for step in range(1, NEAR):
        mean_b_copy(step).start()
    for step in range(1, NEAR):
        mean_b_copy(step).wait_recv()
    part_c[...] = part_b[...] + jnp.sum(got_b[...], axis=0)
    for step in range(1, far_count):
        mean_c_copy(step).start()
    for step in range(1, far_count):
        mean_c_copy(step).wait_recv()
    whole = part_c[...] + jnp.sum(got_c[...], axis=0)
    cells = float(total_rows * total_depth * width)
    mean_ref[...] = jnp.broadcast_to(jnp.sum(whole, axis=1, keepdims=True) / cells, (1, LANES))
    for step in range(1, scen_count):
        mean_a_copy(step).wait_send()
    for step in range(1, NEAR):
        mean_b_copy(step).wait_send()
    for step in range(1, far_count):
        mean_c_copy(step).wait_send()


def solution(mesh):
    scen_count = mesh.shape["scen"]
    grid_count = mesh.shape["grid"]

    def on_device(value_next, scenario_ids, inflow_table, release_shifts, price):
        rows, depth, width = value_next.shape
        tiles = width // LANES
        dims = (scen_count, grid_count, rows, depth, width)
        reach = rows + 2 * H
        vmem = pl.BlockSpec(memory_space=pltpu.VMEM)
        dma = pltpu.SemaphoreType.DMA
        average, mean = pl.pallas_call(
            lambda *refs: kernel(dims, *refs),
            out_shape=(
                jax.ShapeDtypeStruct((rows, depth, width), jnp.float32),
                jax.ShapeDtypeStruct((1, LANES), jnp.float32),
            ),
            in_specs=[pl.BlockSpec(memory_space=pl.ANY)] * 5,
            out_specs=(vmem, vmem),
            scratch_shapes=[
                pltpu.VMEM((tiles, 4, reach, depth, LANES), jnp.float32),
                pltpu.VMEM(((tiles + 2) * reach * 4 * depth, LANES), jnp.float32),
                pltpu.VMEM((1, LANES), jnp.int32),
                pltpu.VMEM((scen_count, 1, LANES), jnp.int32),
                pltpu.VMEM((1, LANES), jnp.float32),
                pltpu.VMEM((scen_count - 1, 1, LANES), jnp.float32),
                pltpu.VMEM((1, LANES), jnp.float32),
                pltpu.VMEM((NEAR - 1, 1, LANES), jnp.float32),
                pltpu.VMEM((1, LANES), jnp.float32),
                pltpu.VMEM((grid_count // NEAR - 1, 1, LANES), jnp.float32),
                pltpu.SMEM((scen_count, 1, LANES), jnp.int32),
                pltpu.SMEM(scenario_ids.shape, jnp.int32),
                pltpu.SMEM(inflow_table.shape[::-1], jnp.int32),
                pltpu.SMEM(release_shifts.shape[::-1], jnp.int32),
                pltpu.SMEM(price.shape, jnp.float32),
                pltpu.SMEM((SCENARIOS * RELEASES,), jnp.int32),
                pltpu.SMEM((SCENARIOS * RELEASES,), jnp.int32),
                pltpu.SMEM((SCENARIOS * RELEASES,), jnp.int32),
                pltpu.SMEM((3 * RELEASES,), jnp.float32),
                dma((tiles,)),
                dma((4,)),
                dma,
                dma((tiles, 4)),
                dma((tiles, 4)),
                dma((tiles, 4, 2)),
                dma((tiles, 4, 2)),
                dma((scen_count - 1,)),
                dma((scen_count - 1,)),
                dma((scen_count - 1,)),
                dma((scen_count - 1,)),
                dma((NEAR - 1,)),
                dma((NEAR - 1,)),
                dma((grid_count // NEAR - 1,)),
                dma((grid_count // NEAR - 1,)),
            ],
            compiler_params=pltpu.CompilerParams(
                collective_id=0, has_side_effects=True, vmem_limit_bytes=40 * 1024 * 1024
            ),
        )(value_next, scenario_ids, inflow_table.T, release_shifts.T, price)
        return average - mean[0, 0]

    return jax.shard_map(
        on_device,
        mesh=mesh,
        in_specs=(P("grid", "scen", None), P("scen"), P(), P(), P()),
        out_specs=P("grid", "scen", None),
        check_vma=False,
    )
```

time: 141 us -> 75.2 us (0.53)
  Pallas kernels: 137 us -> 71.7 us
    pallas_call x1, Pallas kernels: 137 us -> 71.7 us  [on_device(): pl.pallas_call(lambda *refs: kernel(dims, *refs), out_shape=(jax.ShapeDty...]
where the time goes in v2:
time: 75.2 us; the launch traced here: 75 us
  Pallas kernels  71.7 us (95%)
  local copies, waits for them, and re-layouts  1.7 us (2%)
  other arithmetic  0.87 us (1%)
    pallas_call x1, Pallas kernels, on_device(): pl.pallas_call(lambda *refs: kernel(dims, *refs), out_shape=(jax.ShapeDty...  71.7 us
    unnamed x8, local copies, waits for them, and re-layouts  1.7 us

profile of v2, /device:TPU:1, one launch (start us, length us, event | category | flops | bytes accessed | tf_op | source)
XLA Modules:
  0.0 75.0 jit_solution(6043287750272135028)
XLA Ops:
  0.0 0.0 copy-start.2
  0.7 0.0 copy-start.1
  0.7 0.0 copy-start.3
  0.7 0.0 copy-done.2
  0.7 0.7 copy-done.1
  1.4 0.0 copy-done.3
  1.4 0.0 copy-start
  1.4 1.0 %copy-done = f32[16,8,1024]{2,1,0:T(8,128)S(1)} copy-done((f32[16,8,1024]{2,1,0:T(8,128)S(1)}, f32[16,8,1024]{2,1,0:T(8,128)}, u32[]{:S(2)}) %copy-start) | copy-done | bytes 524312
  2.4 71.7 %shard_map.55 = (f32[16,8,1024]{2,1,0:T(8,128)S(1)}, f32[1,128]{1,0:T(1,128)S(1)}) custom-call(f32[16,8,1024]{2,1,0:T(8,128)S(1)} %copy-done, s32[1]{0:T(128)S(6)} %copy.6.refs_1_, s32[3,12]{1,0:T(4,128)S(1)} %bitcast.4, s32[3,16]{1,0:T(4,128)S(1)} %bitcast.5, f32[3]{0:T(128)S(1)} %copy-done.3), custom_call_target="tpu_custom_call" | custom-call | tf_op jit(solution)/shard_map/pallas_call | solution.py:521
  74.1 0.9 %broadcast_subtract_fusion = f32[16,8,1024]{2,1,0:T(8,128)} fusion(f32[16,8,1024]{2,1,0:T(8,128)S(1)} %get-tuple-element.7, f32[]{:T(128)S(1)} %bitcast.6), kind=kLoop, calls=%fused_computation | loop fusion | flops 131072 | bytes 1048580 | tf_op jit(solution)/shard_map/sub | solution.py:569
Async XLA Ops:
  0.0 0.7 copy-start.2
  0.7 0.7 copy-start.1
  0.7 0.7 copy-start.3
  1.4 1.0 %copy-start = (f32[16,8,1024]{2,1,0:T(8,128)S(1)}, f32[16,8,1024]{2,1,0:T(8,128)}, u32[]{:S(2)}) copy-start(f32[16,8,1024]{2,1,0:T(8,128)} %refs_0_.1) | copy-start | bytes 1572868

commit v3 on v2

v3 whole, which is shorter than its diff:
```python
import math

import jax
import jax.numpy as jnp
from jax import lax
from jax.experimental import pallas as pl
from jax.experimental.pallas import tpu as pltpu
from jax.sharding import PartitionSpec as P

H = 8
RELEASES = 16
SCENARIOS = 8
LANES = 128
LOG2E = 1.4426950408889634
MESH = pl.DeviceIdType.MESH
NEAR = 8


def kernel(
    dims,
    x_ref,
    id_hbm,
    inflow_hbm,
    release_hbm,
    price_hbm,
    avg_ref,
    mean_ref,
    held,
    packed,
    raw,
    side,
    grown,
    outgoing,
    result,
    own_id,
    all_ids,
    part_a,
    got_a,
    part_b,
    got_b,
    part_c,
    got_c,
    ids_s,
    id_ref,
    inflow_ref,
    release_ref,
    price_ref,
    base_s,
    other_s,
    amount_s,
    turn_s,
    rate_s,
    held_sem,
    local_sem,
    small_sem,
    send_x,
    recv_x,
    send_y,
    recv_y,
    send_a,
    recv_a,
    send_b,
    recv_b,
    send_o,
    recv_o,
    send_id,
    recv_id,
    send_ma,
    recv_ma,
    send_mb,
    recv_mb,
    send_mc,
    recv_mc,
):
    scen_count, grid_count, rows, depth, width = dims
    total_rows = rows * grid_count
    total_depth = depth * scen_count
    span = total_depth + 3 * depth
    reach = rows + 2 * H
    tile_rows = reach * span
    pack = 4
    s = lax.axis_index("scen")
    g = lax.axis_index("grid")
    near = lax.rem(g, NEAR)
    far_count = grid_count // NEAR

    def scen_index(step):
        return lax.rem(s + step + scen_count, scen_count)

    def scen_peer(step):
        return {"scen": scen_index(step), "grid": g}

    def grid_peer(step):
        return {"scen": s, "grid": lax.rem(g + step + grid_count, grid_count)}

    def near_peer(step):
        return {"scen": s, "grid": g - near + lax.rem(near + step, NEAR)}

    def lanes(i):
        return pl.ds(pl.multiple_of(i * LANES, LANES), LANES)

    def remote(source, target, send_sem, recv_sem, peer):
        return pltpu.make_async_remote_copy(
            src_ref=source,
            dst_ref=target,
            send_sem=send_sem,
            recv_sem=recv_sem,
            device_id=peer,
            device_id_type=MESH,
        )

    def tile_copy(step):
        return remote(
            x_ref.at[:, :, lanes(scen_index(step))],
            raw.at[s, pl.ds(H, rows)],
            send_x.at[step - 1],
            recv_x.at[step - 1],
            scen_peer(step),
        )

    def side_copy(step):
        return remote(
            packed.at[scen_index(step)],
            side.at[s, pl.ds(H // pack, rows // pack)],
            send_y.at[step - 1],
            recv_y.at[step - 1],
            scen_peer(step),
        )

    def row_copy(step, way):
        q = scen_index(-step)
        first, landing, to = ((H, H + rows, -1), (rows, 0, 1))[way]
        return remote(
            raw.at[q, pl.ds(first, H)],
            raw.at[q, pl.ds(landing, H)],
            send_a.at[step, way],
            recv_a.at[step, way],
            grid_peer(to),
        )

    def row_side_copy(step, way):
        q = scen_index(-step)
        first, landing, to = ((H, H + rows, -1), (rows, 0, 1))[way]
        return remote(
            side.at[q, pl.ds(first // pack, H // pack)],
            side.at[q, pl.ds(landing // pack, H // pack)],
            send_b.at[step, way],
            recv_b.at[step, way],
            grid_peer(to),
        )

    def out_copy(step):
        return remote(
            outgoing.at[scen_index(step)],
            result.at[s],
            send_o.at[step - 1],
            recv_o.at[step - 1],
            scen_peer(step),
        )

    def id_copy(step):
        return remote(
            own_id, all_ids.at[s], send_id.at[step - 1], recv_id.at[step - 1], scen_peer(step)
        )

    def mean_a_copy(step):
        return remote(
            part_a, got_a.at[step - 1], send_ma.at[step - 1], recv_ma.at[step - 1], scen_peer(step)
        )

    def mean_b_copy(step):
        return remote(
            part_b, got_b.at[step - 1], send_mb.at[step - 1], recv_mb.at[step - 1], near_peer(step)
        )

    def mean_c_copy(step):
        return remote(
            part_c,
            got_c.at[step - 1],
            send_mc.at[step - 1],
            recv_mc.at[step - 1],
            grid_peer(step * NEAR),
        )

    def loop(start, stop, body):
        def step(i, carry):
            body(i)
            return carry

        lax.fori_loop(start, stop, step, 0)

    barrier = pltpu.get_barrier_semaphore()

    def greet(peer):
        pl.semaphore_signal(barrier, inc=1, device_id=peer, device_id_type=MESH)

    for step in range(1, scen_count):
        greet(scen_peer(step))
    for step in range(1, NEAR):
        greet(near_peer(step))
    for step in range(1, far_count):
        greet(grid_peer(step * NEAR))
    for step in (-1, 1):
        greet(grid_peer(step))

    to_held = pltpu.make_async_copy(x_ref, held, held_sem)
    to_held.start()
    small = [
        pltpu.make_async_copy(source, target, small_sem.at[n])
        for n, (source, target) in enumerate(
            ((id_hbm, id_ref), (inflow_hbm, inflow_ref), (release_hbm, release_ref), (price_hbm, price_ref))
        )
    ]
    for copy in small:
        copy.start()
    own_tile = pltpu.make_async_copy(
        x_ref.at[:, :, lanes(s)], raw.at[s, pl.ds(H, rows)], local_sem.at[0]
    )
    own_tile.start()
    for copy in small:
        copy.wait()
    own_id[...] = jnp.full((1, LANES), id_ref[0], jnp.int32)
    all_ids[s] = jnp.full((1, LANES), id_ref[0], jnp.int32)

    lane = lax.broadcasted_iota(jnp.int32, (depth, LANES), 1)
    to_held.wait()

    def pack_group(p):
        for k in range(scen_count):
            together = None
            for r in range(pack):
                a = p * pack + r
                if k > 0:
                    before = held[a, :, (k - 1) * LANES : k * LANES]
                else:
                    before = jnp.broadcast_to(held[a, :, 0:LANES][:, 0:1], (depth, LANES))
                if k < scen_count - 1:
                    after = held[a, :, (k + 1) * LANES : (k + 2) * LANES]
                else:
                    last = held[a, :, k * LANES : (k + 1) * LANES]
                    after = jnp.broadcast_to(last[:, LANES - 1 : LANES], (depth, LANES))
                both = jnp.where(lane < LANES // 2, after, before)
                if r == 0:
                    together = both
                else:
                    mine = jnp.bitwise_and(lane - 32 * r + H, LANES - 1) < 3 * H
                    together = jnp.where(mine, pltpu.roll(both, 32 * r, 1), together)
            packed[k, p] = together

    loop(0, rows // pack, pack_group)
    own_side = pltpu.make_async_copy(
        packed.at[s], side.at[s, pl.ds(H // pack, rows // pack)], local_sem.at[1]
    )
    own_side.start()

    pl.semaphore_wait(barrier, scen_count + NEAR + far_count - 1)
    order = (4, 3, 5, 2, 6, 1, 7)
    for step in order:
        tile_copy(step).start()
        side_copy(step).start()
    for step in range(1, scen_count):
        id_copy(step).start()

    def pass_rows(step):
        for way in (0, 1):
            row_copy(step, way).start()
            row_side_copy(step, way).start()

    own_tile.wait()
    own_side.wait()
    pass_rows(0)

    scale = -LOG2E / 4.0

    def rates(r):
        rate_s[r] = (price_ref[0] * scale / total_rows) * (H - release_ref[0, r]).astype(jnp.float32)
        rate_s[RELEASES + r] = (price_ref[1] * scale / width) * (H - release_ref[1, r]).astype(jnp.float32)
        rate_s[2 * RELEASES + r] = (price_ref[2] * scale / total_depth) * (H - release_ref[2, r]).astype(
            jnp.float32
        )

    loop(0, RELEASES, rates)

    for step in range(1, scen_count):
        id_copy(step).wait_recv()
    to_scalar = pltpu.make_async_copy(all_ids, ids_s, local_sem.at[2])
    to_scalar.start()
    to_scalar.wait()

    def shifts(w):
        row = ids_s[w, 0, 0]
        i1 = inflow_ref[0, row]
        i2 = inflow_ref[1, row]
        i3 = inflow_ref[2, row]

        def one(r):
            u1 = release_ref[0, r]
            u2 = release_ref[1, r]
            u3 = release_ref[2, r]
            along = i2 + u1 - u2
            back = jnp.where(along < 0, 1, 0)
            at = r * SCENARIOS + w
            amount = along + back * LANES
            base_s[at] = back * tile_rows + (H + i1 - u1) * span + (depth + i3 + u2 - u3)
            other_s[at] = (1 - back) * tile_rows + (H + i1 - u1) * span + (depth + i3 + u2 - u3)
            amount_s[at] = amount
            turn_s[at] = jnp.bitwise_and(LANES - amount, LANES - 1)

        loop(0, RELEASES, one)

    loop(0, scen_count, shifts)

    for step in order:
        tile_copy(step).wait_recv()
        side_copy(step).wait_recv()
        pass_rows(step)

    lowest = jnp.where(g == 0, H, 0)
    highest = jnp.where(g == grid_count - 1, H + rows - 1, reach - 1)

    def grow(v):
        return jnp.exp2(v * (-2.0 * LOG2E))

    def build(q):
        def some_rows(block):
            for k in range(4):
                a = block * 4 + k
                source = jnp.clip(a, lowest, highest)
                at = pl.multiple_of(a * span + (q + 1) * depth, depth)
                grown[pl.ds(at, depth), :] = grow(raw[q, source])
                turned = jnp.bitwise_and(LANES - 32 * lax.rem(source, pack), LANES - 1)
                grown[pl.ds(tile_rows + at, depth), :] = grow(
                    pltpu.roll(side[q, source // pack], turned, 1)
                )

        loop(0, reach // 4, some_rows)

    def build_step(step):
        for way in (0, 1):
            row_copy(step, way).wait_recv()
            row_side_copy(step, way).wait_recv()
        build(scen_index(-step))

    build_step(0)
    for step in order:
        build_step(step)

    def outer(block):
        for k in range(4):
            row = (block * 4 + k) * span
            low = grown[pl.ds(pl.multiple_of(row + depth, depth), depth), :]
            high = grown[pl.ds(pl.multiple_of(row + total_depth, depth), depth), :]
            grown[pl.ds(pl.multiple_of(row, depth), depth), :] = jnp.broadcast_to(low[0:1], low.shape)
            top = jnp.broadcast_to(high[depth - 1 : depth], low.shape)
            for extra in (1, 2):
                at = pl.multiple_of(row + total_depth + extra * depth, depth)
                grown[pl.ds(at, depth), :] = top

    loop(0, 2 * reach // 4, outer)

    group = 4
    level_b = (lane + s * LANES + 1).astype(jnp.float32)
    level_in = lax.broadcasted_iota(jnp.int32, (depth, LANES), 0) + 1

    def compute(q, step, total):
        t = scen_index(step)
        first = q * group
        offset = t * depth + first * span
        level_c = (level_in + t * depth).astype(jnp.float32)
        sums = [jnp.zeros((depth, LANES), jnp.float32)] * (SCENARIOS * group)
        for r in range(RELEASES):
            flat = rate_s[2 * RELEASES + r] * level_c + rate_s[RELEASES + r] * level_b
            weights = []
            for k in range(group):
                row = (g * rows + first + k + 1).astype(jnp.float32)
                weights.append(jnp.exp2(flat + rate_s[r] * row))
            for w in range(SCENARIOS):
                at = base_s[r * SCENARIOS + w] + offset
                other = other_s[r * SCENARIOS + w] + offset
                mask = lane < amount_s[r * SCENARIOS + w]
                turn = turn_s[r * SCENARIOS + w]
                for k in range(group):
                    low = grown[pl.ds(at + k * span, depth), :]
                    high = grown[pl.ds(other + k * span, depth), :]
                    landed = pltpu.roll(jnp.where(mask, high, low), turn, 1)
                    sums[w * group + k] = sums[w * group + k] + weights[k] * landed
        for k in range(group):
            v = [sums[w * group + k] for w in range(SCENARIOS)]
            logs = jnp.log(v[0] * v[1] * (v[2] * v[3])) + jnp.log(v[4] * v[5] * (v[6] * v[7]))
            row = (g * rows + first + k + 1).astype(jnp.float32)
            top = (
                (price_ref[2] / total_depth) * level_c
                + (price_ref[1] / width) * level_b
                + (price_ref[0] / total_rows) * row
            )
            value = -top - (0.5 / SCENARIOS) * logs
            outgoing[t, first + k] = value
            total = total + value
        return total

    def part(n, total):
        step = 1 + n // (rows // group)
        q = lax.rem(n, rows // group)

        @pl.when(jnp.logical_and(q == 1, step >= 2))
        def _():
            out_copy(step - 1).start()

        return compute(q, step, total)

    total = jnp.zeros((depth, LANES), jnp.float32)
    total = lax.fori_loop(0, scen_count * (rows // group), part, total)

    part_a[...] = jnp.sum(total, axis=0, keepdims=True)
    for step in range(1, scen_count):
        mean_a_copy(step).start()
    for step in range(1, scen_count):
        id_copy(step).wait_send()
        tile_copy(step).wait_send()
        side_copy(step).wait_send()
    for step in range(scen_count):
        for way in (0, 1):
            row_copy(step, way).wait_send()
            row_side_copy(step, way).wait_send()
    for step in range(1, scen_count):
        mean_a_copy(step).wait_recv()
    part_b[...] = part_a[...] + jnp.sum(got_a[...], axis=0)
    for step in range(1, NEAR):
        mean_b_copy(step).start()
    result[s] = outgoing[s]
    for step in range(1, scen_count):
        out_copy(step).wait_recv()
        out_copy(step).wait_send()
    for k in range(scen_count):
        avg_ref[:, :, k * LANES : (k + 1) * LANES] = result[k]
    for step in range(1, NEAR):
        mean_b_copy(step).wait_recv()
    part_c[...] = part_b[...] + jnp.sum(got_b[...], axis=0)
    for step in range(1, far_count):
        mean_c_copy(step).start()
    for step in range(1, scen_count):
        mean_a_copy(step).wait_send()
    for step in range(1, NEAR):
        mean_b_copy(step).wait_send()
    for step in range(1, far_count):
        mean_c_copy(step).wait_recv()
    whole = part_c[...] + jnp.sum(got_c[...], axis=0)
    cells = float(total_rows * total_depth * width)
    mean_ref[...] = jnp.broadcast_to(jnp.sum(whole, axis=1, keepdims=True) / cells, (1, LANES))
    for step in range(1, far_count):
        mean_c_copy(step).wait_send()


def solution(mesh):
    scen_count = mesh.shape["scen"]
    grid_count = mesh.shape["grid"]

    def on_device(value_next, scenario_ids, inflow_table, release_shifts, price):
        rows, depth, width = value_next.shape
        dims = (scen_count, grid_count, rows, depth, width)
        reach = rows + 2 * H
        span = depth * (scen_count + 3)
        far_count = grid_count // NEAR
        vmem = pl.BlockSpec(memory_space=pltpu.VMEM)
        dma = pltpu.SemaphoreType.DMA
        peers = scen_count - 1
        f32, i32 = jnp.float32, jnp.int32
        average, mean = pl.pallas_call(
            lambda *refs: kernel(dims, *refs),
            out_shape=(
                jax.ShapeDtypeStruct((rows, depth, width), f32),
                jax.ShapeDtypeStruct((1, LANES), f32),
            ),
            in_specs=[pl.BlockSpec(memory_space=pl.ANY)] * 5,
            out_specs=(vmem, vmem),
            scratch_shapes=[
                pltpu.VMEM((rows, depth, width), f32),
                pltpu.VMEM((scen_count, rows // 4, depth, LANES), f32),
                pltpu.VMEM((scen_count, reach, depth, LANES), f32),
                pltpu.VMEM((scen_count, reach // 4, depth, LANES), f32),
                pltpu.VMEM((2 * reach * span, LANES), f32),
                pltpu.VMEM((scen_count, rows, depth, LANES), f32),
                pltpu.VMEM((scen_count, rows, depth, LANES), f32),
                pltpu.VMEM((1, LANES), i32),
                pltpu.VMEM((scen_count, 1, LANES), i32),
                pltpu.VMEM((1, LANES), f32),
                pltpu.VMEM((peers, 1, LANES), f32),
                pltpu.VMEM((1, LANES), f32),
                pltpu.VMEM((NEAR - 1, 1, LANES), f32),
                pltpu.VMEM((1, LANES), f32),
                pltpu.VMEM((far_count - 1, 1, LANES), f32),
                pltpu.SMEM((scen_count, 1, LANES), i32),
                pltpu.SMEM(scenario_ids.shape, i32),
                pltpu.SMEM(inflow_table.shape[::-1], i32),
                pltpu.SMEM(release_shifts.shape[::-1], i32),
                pltpu.SMEM(price.shape, f32),
                pltpu.SMEM((SCENARIOS * RELEASES,), i32),
                pltpu.SMEM((SCENARIOS * RELEASES,), i32),
                pltpu.SMEM((SCENARIOS * RELEASES,), i32),
                pltpu.SMEM((SCENARIOS * RELEASES,), i32),
                pltpu.SMEM((3 * RELEASES,), f32),
                dma,
                dma((3,)),
                dma((4,)),
                dma((peers,)),
                dma((peers,)),
                dma((peers,)),
                dma((peers,)),
                dma((scen_count, 2)),
                dma((scen_count, 2)),
                dma((scen_count, 2)),
                dma((scen_count, 2)),
                dma((peers,)),
                dma((peers,)),
                dma((peers,)),
                dma((peers,)),
                dma((peers,)),
                dma((peers,)),
                dma((NEAR - 1,)),
                dma((NEAR - 1,)),
                dma((far_count - 1,)),
                dma((far_count - 1,)),
            ],
            compiler_params=pltpu.CompilerParams(
                collective_id=0, has_side_effects=True, vmem_limit_bytes=60 * 1024 * 1024
            ),
        )(value_next, scenario_ids, inflow_table.T, release_shifts.T, price)
        return average - mean[0, 0]

    return jax.shard_map(
        on_device,
        mesh=mesh,
        in_specs=(P("grid", "scen", None), P("scen"), P(), P(), P()),
        out_specs=P("grid", "scen", None),
        check_vma=False,
    )
```

time: 75.2 us -> 74.6 us (level)
  Pallas kernels: 71.7 us -> 70.5 us
  other arithmetic: 0.87 us -> 1.92 us
  local copies, waits for them, and re-layouts: 1.7 us -> 0.66 us
    pallas_call x1, Pallas kernels: 71.7 us -> 70.5 us  [on_device(): pl.pallas_call(lambda *refs: kernel(dims, *refs), out_shape=(jax.ShapeDty...]
    sub x1, other arithmetic: 0.87 us -> 1.92 us  [on_device(): return average - mean[0, 0]]
    unnamed x8 -> x2, local copies, waits for them, and re-layouts: 1.7 us -> 0.66 us
where the time goes in v3:
time: 74.6 us; the launch traced here: 73.8 us
  Pallas kernels  70.5 us (95%)
  other arithmetic  1.92 us (3%)
    pallas_call x1, Pallas kernels, on_device(): pl.pallas_call(lambda *refs: kernel(dims, *refs), out_shape=(jax.ShapeDty...  70.5 us
    sub x1, other arithmetic, on_device(): return average - mean[0, 0]  1.92 us

profile of v3, /device:TPU:1, one launch (start us, length us, event | category | flops | bytes accessed | tf_op | source)
XLA Modules:
  0.0 73.8 jit_solution(1164447087670507361)
XLA Ops:
  0.7 70.5 %shard_map.55 = (f32[16,8,1024]{2,1,0:T(8,128)}, f32[1,128]{1,0:T(1,128)}) custom-call(f32[16,8,1024]{2,1,0:T(8,128)} %refs_0_.1, s32[1]{0:T(128)S(6)} %copy.6.refs_1_, s32[3,12]{1,0:T(4,128)} %bitcast.4, s32[3,16]{1,0:T(4,128)} %bitcast.5, f32[3]{0:T(128)} %refs_4_.1), custom_call_target="tpu_custom_call" | custom-call | tf_op jit(solution)/shard_map/pallas_call | solution.py:468
  71.2 0.0 copy-start
  71.2 0.7 copy-done
  71.9 1.9 %broadcast_subtract_fusion = f32[16,8,1024]{2,1,0:T(8,128)} fusion(f32[16,8,1024]{2,1,0:T(8,128)} %get-tuple-element.7, f32[]{:T(128)S(1)} %bitcast.6), kind=kLoop, calls=%fused_computation | loop fusion | flops 131072 | bytes 1048580 | tf_op jit(solution)/shard_map/sub | solution.py:528
Async XLA Ops:
  71.2 0.7 copy-start

commit v4 on v3

--- a/solution.py
+++ b/solution.py
@@ -254,7 +254,7 @@
     own_side.start()
 
     pl.semaphore_wait(barrier, scen_count + NEAR + far_count - 1)
-    order = (4, 3, 5, 2, 6, 1, 7)
+    order = (1, 7, 6, 5, 4, 3, 2)
     for step in order:
         tile_copy(step).start()
         side_copy(step).start()
@@ -269,6 +269,15 @@
     own_tile.wait()
     own_side.wait()
     pass_rows(0)
+
+    def take(step):
+        tile_copy(step).wait_recv()
+        side_copy(step).wait_recv()
+        pass_rows(step)
+
+    early = 3
+    for step in order[:early]:
+        take(step)
 
     scale = -LOG2E / 4.0
 
@@ -310,10 +319,8 @@
 
     loop(0, scen_count, shifts)
 
-    for step in order:
-        tile_copy(step).wait_recv()
-        side_copy(step).wait_recv()
-        pass_rows(step)
+    for step in order[early:]:
+        take(step)
 
     lowest = jnp.where(g == 0, H, 0)
     highest = jnp.where(g == grid_count - 1, H + rows - 1, reach - 1)
@@ -335,28 +342,39 @@
 
         loop(0, reach // 4, some_rows)
 
+        @pl.when(q == 0)
+        def _():
+            def below(block):
+                for k in range(8):
+                    row = (block * 8 + k) * span
+                    low = grown[pl.ds(pl.multiple_of(row + depth, depth), depth), :]
+                    grown[pl.ds(pl.multiple_of(row, depth), depth), :] = jnp.broadcast_to(
+                        low[0:1], low.shape
+                    )
+
+            loop(0, 2 * reach // 8, below)
+
+        @pl.when(q == scen_count - 1)
+        def _():
+            def above(block):
+                for k in range(8):
+                    row = (block * 8 + k) * span
+                    high = grown[pl.ds(pl.multiple_of(row + total_depth, depth), depth), :]
+                    top = jnp.broadcast_to(high[depth - 1 : depth], high.shape)
+                    for extra in (1, 2):
+                        at = pl.multiple_of(row + total_depth + extra * depth, depth)
+                        grown[pl.ds(at, depth), :] = top
+
+            loop(0, 2 * reach // 8, above)
+
     def build_step(step):
         for way in (0, 1):
             row_copy(step, way).wait_recv()
             row_side_copy(step, way).wait_recv()
         build(scen_index(-step))
 
-    build_step(0)
-    for step in order:
-        build_step(step)
-
-    def outer(block):
-        for k in range(4):
-            row = (block * 4 + k) * span
-            low = grown[pl.ds(pl.multiple_of(row + depth, depth), depth), :]
-            high = grown[pl.ds(pl.multiple_of(row + total_depth, depth), depth), :]
-            grown[pl.ds(pl.multiple_of(row, depth), depth), :] = jnp.broadcast_to(low[0:1], low.shape)
-            top = jnp.broadcast_to(high[depth - 1 : depth], low.shape)
-            for extra in (1, 2):
-                at = pl.multiple_of(row + total_depth + extra * depth, depth)
-                grown[pl.ds(at, depth), :] = top
-
-    loop(0, 2 * reach // 4, outer)
+    loop(0, 2, build_step)
+    loop(scen_count - 2, scen_count, build_step)
 
     group = 4
     level_b = (lane + s * LANES + 1).astype(jnp.float32)
@@ -399,8 +417,12 @@
         return total
 
     def part(n, total):
-        step = 1 + n // (rows // group)
+        step = n // (rows // group)
         q = lax.rem(n, rows // group)
+
+        @pl.when(jnp.logical_and(q == 0, jnp.logical_and(step >= 1, step <= scen_count - 4)))
+        def _():
+            build_step(scen_count - 2 - step)
 
         @pl.when(jnp.logical_and(q == 1, step >= 2))
         def _():
@@ -414,6 +436,7 @@
     part_a[...] = jnp.sum(total, axis=0, keepdims=True)
     for step in range(1, scen_count):
         mean_a_copy(step).start()
+    out_copy(scen_count - 1).start()
     for step in range(1, scen_count):
         id_copy(step).wait_send()
         tile_copy(step).wait_send()
@@ -471,7 +494,7 @@
                 jax.ShapeDtypeStruct((rows, depth, width), f32),
                 jax.ShapeDtypeStruct((1, LANES), f32),
             ),
-            in_specs=[pl.BlockSpec(memory_space=pl.ANY)] * 5,
+            in_specs=[pl.BlockSpec(memory_space=pltpu.HBM)] * 5,
             out_specs=(vmem, vmem),
             scratch_shapes=[
                 pltpu.VMEM((rows, depth, width), f32),
@@ -522,7 +545,7 @@
                 dma((far_count - 1,)),
             ],
             compiler_params=pltpu.CompilerParams(
-                collective_id=0, has_side_effects=True, vmem_limit_bytes=60 * 1024 * 1024
+                collective_id=0, has_side_effects=True, vmem_limit_bytes=24 * 1024 * 1024
             ),
         )(value_next, scenario_ids, inflow_table.T, release_shifts.T, price)
         return average - mean[0, 0]

time: 74.6 us -> 70.1 us (0.940)
  Pallas kernels: 70.5 us -> 66.7 us
  other arithmetic: 1.92 us -> 0.87 us
  local copies, waits for them, and re-layouts: 0.66 us -> 1.7 us
    pallas_call x1, Pallas kernels: 70.5 us -> 66.7 us  [on_device(): pl.pallas_call(lambda *refs: kernel(dims, *refs), out_shape=(jax.ShapeDty...]
    sub x1, other arithmetic: 1.92 us -> 0.87 us  [on_device(): return average - mean[0, 0]]
    unnamed x2 -> x8, local copies, waits for them, and re-layouts: 0.66 us -> 1.7 us
where the time goes in v4:
time: 70.1 us; the launch traced here: 70 us
  Pallas kernels  66.7 us (95%)
  local copies, waits for them, and re-layouts  1.7 us (2%)
  other arithmetic  0.87 us (1%)
    pallas_call x1, Pallas kernels, on_device(): pl.pallas_call(lambda *refs: kernel(dims, *refs), out_shape=(jax.ShapeDty...  66.7 us
    unnamed x8, local copies, waits for them, and re-layouts  1.7 us

profile of v4, /device:TPU:1, one launch (start us, length us, event | category | flops | bytes accessed | tf_op | source)
XLA Modules:
  0.0 70.0 jit_solution(5675098610681720244)
XLA Ops:
  0.0 0.0 copy-start.2
  0.7 0.0 copy-start.1
  0.7 0.0 copy-start.3
  0.7 0.0 copy-done.2
  0.7 0.7 copy-done.1
  1.4 0.0 copy-done.3
  1.4 0.0 copy-start
  1.4 1.0 %copy-done = f32[16,8,1024]{2,1,0:T(8,128)S(1)} copy-done((f32[16,8,1024]{2,1,0:T(8,128)S(1)}, f32[16,8,1024]{2,1,0:T(8,128)}, u32[]{:S(2)}) %copy-start) | copy-done | bytes 524312
  2.4 66.7 %shard_map.55 = (f32[16,8,1024]{2,1,0:T(8,128)S(1)}, f32[1,128]{1,0:T(1,128)S(1)}) custom-call(f32[16,8,1024]{2,1,0:T(8,128)S(1)} %copy-done, s32[1]{0:T(128)S(6)} %copy.6.refs_1_, s32[3,12]{1,0:T(4,128)S(1)} %bitcast.4, s32[3,16]{1,0:T(4,128)S(1)} %bitcast.5, f32[3]{0:T(128)S(1)} %copy-done.3), custom_call_target="tpu_custom_call" | custom-call | tf_op jit(solution)/shard_map/pallas_call | solution.py:491
  69.1 0.9 %broadcast_subtract_fusion = f32[16,8,1024]{2,1,0:T(8,128)} fusion(f32[16,8,1024]{2,1,0:T(8,128)S(1)} %get-tuple-element.7, f32[]{:T(128)S(1)} %bitcast.6), kind=kLoop, calls=%fused_computation | loop fusion | flops 131072 | bytes 1048580 | tf_op jit(solution)/shard_map/sub | solution.py:551
Async XLA Ops:
  0.0 0.7 copy-start.2
  0.7 0.7 copy-start.1
  0.7 0.7 copy-start.3
  1.4 1.0 %copy-start = (f32[16,8,1024]{2,1,0:T(8,128)S(1)}, f32[16,8,1024]{2,1,0:T(8,128)}, u32[]{:S(2)}) copy-start(f32[16,8,1024]{2,1,0:T(8,128)} %refs_0_.1) | copy-start | bytes 1572868

commit v5 on v4

--- a/solution.py
+++ b/solution.py
@@ -8,6 +8,7 @@
 from jax.sharding import PartitionSpec as P
 
 H = 8
+SHIFTS = 3 * H + 1
 RELEASES = 16
 SCENARIOS = 8
 LANES = 128
@@ -46,9 +47,6 @@
     release_ref,
     price_ref,
     base_s,
-    other_s,
-    amount_s,
-    turn_s,
     rate_s,
     held_sem,
     local_sem,
@@ -306,21 +304,15 @@
             u1 = release_ref[0, r]
             u2 = release_ref[1, r]
             u3 = release_ref[2, r]
-            along = i2 + u1 - u2
-            back = jnp.where(along < 0, 1, 0)
-            at = r * SCENARIOS + w
-            amount = along + back * LANES
-            base_s[at] = back * tile_rows + (H + i1 - u1) * span + (depth + i3 + u2 - u3)
-            other_s[at] = (1 - back) * tile_rows + (H + i1 - u1) * span + (depth + i3 + u2 - u3)
-            amount_s[at] = amount
-            turn_s[at] = jnp.bitwise_and(LANES - amount, LANES - 1)
+            copy = H + i2 + u1 - u2
+            base_s[r * SCENARIOS + w] = (
+                copy * tile_rows + (H + i1 - u1) * span + (depth + i3 + u2 - u3)
+            )
 
         loop(0, RELEASES, one)
 
     loop(0, scen_count, shifts)
 
-    for step in order[early:]:
-        take(step)
 
     lowest = jnp.where(g == 0, H, 0)
     highest = jnp.where(g == grid_count - 1, H + rows - 1, reach - 1)
@@ -334,11 +326,20 @@
                 a = block * 4 + k
                 source = jnp.clip(a, lowest, highest)
                 at = pl.multiple_of(a * span + (q + 1) * depth, depth)
-                grown[pl.ds(at, depth), :] = grow(raw[q, source])
+                main = grow(raw[q, source])
                 turned = jnp.bitwise_and(LANES - 32 * lax.rem(source, pack), LANES - 1)
-                grown[pl.ds(tile_rows + at, depth), :] = grow(
-                    pltpu.roll(side[q, source // pack], turned, 1)
-                )
+                beside = grow(pltpu.roll(side[q, source // pack], turned, 1))
+                for copy in range(SHIFTS):
+                    shift = copy - H
+                    if shift == 0:
+                        moved = main
+                    elif shift > 0:
+                        moved = pltpu.roll(jnp.where(lane < shift, beside, main), LANES - shift, 1)
+                    else:
+                        moved = pltpu.roll(
+                            jnp.where(lane >= LANES + shift, beside, main), -shift, 1
+                        )
+                    grown[pl.ds(copy * tile_rows + at, depth), :] = moved
 
         loop(0, reach // 4, some_rows)
 
@@ -347,25 +348,25 @@
             def below(block):
                 for k in range(8):
                     row = (block * 8 + k) * span
-                    low = grown[pl.ds(pl.multiple_of(row + depth, depth), depth), :]
+                    low = grown[pl.ds(pl.multiple_of(row + depth, depth), 1), :]
                     grown[pl.ds(pl.multiple_of(row, depth), depth), :] = jnp.broadcast_to(
-                        low[0:1], low.shape
+                        low, (depth, LANES)
                     )
 
-            loop(0, 2 * reach // 8, below)
+            loop(0, SHIFTS * reach // 8, below)
 
         @pl.when(q == scen_count - 1)
         def _():
             def above(block):
                 for k in range(8):
                     row = (block * 8 + k) * span
-                    high = grown[pl.ds(pl.multiple_of(row + total_depth, depth), depth), :]
-                    top = jnp.broadcast_to(high[depth - 1 : depth], high.shape)
+                    high = grown[pl.ds(row + total_depth + depth - 1, 1), :]
+                    top = jnp.broadcast_to(high, (depth, LANES))
                     for extra in (1, 2):
                         at = pl.multiple_of(row + total_depth + extra * depth, depth)
                         grown[pl.ds(at, depth), :] = top
 
-            loop(0, 2 * reach // 8, above)
+            loop(0, SHIFTS * reach // 8, above)
 
     def build_step(step):
         for way in (0, 1):
@@ -373,8 +374,11 @@
             row_side_copy(step, way).wait_recv()
         build(scen_index(-step))
 
-    loop(0, 2, build_step)
-    loop(scen_count - 2, scen_count, build_step)
+    build_step(0)
+    for n, step in enumerate(order[early:]):
+        take(step)
+        if n < early:
+            build_step(order[n])
 
     group = 4
     level_b = (lane + s * LANES + 1).astype(jnp.float32)
@@ -385,8 +389,8 @@
         first = q * group
         offset = t * depth + first * span
         level_c = (level_in + t * depth).astype(jnp.float32)
-        sums = [jnp.zeros((depth, LANES), jnp.float32)] * (SCENARIOS * group)
-        for r in range(RELEASES):
+        def one_release(r, sums):
+            sums = list(sums)
             flat = rate_s[2 * RELEASES + r] * level_c + rate_s[RELEASES + r] * level_b
             weights = []
             for k in range(group):
@@ -394,14 +398,14 @@
                 weights.append(jnp.exp2(flat + rate_s[r] * row))
             for w in range(SCENARIOS):
                 at = base_s[r * SCENARIOS + w] + offset
-                other = other_s[r * SCENARIOS + w] + offset
-                mask = lane < amount_s[r * SCENARIOS + w]
-                turn = turn_s[r * SCENARIOS + w]
                 for k in range(group):
-                    low = grown[pl.ds(at + k * span, depth), :]
-                    high = grown[pl.ds(other + k * span, depth), :]
-                    landed = pltpu.roll(jnp.where(mask, high, low), turn, 1)
+                    landed = grown[pl.ds(at + k * span, depth), :]
                     sums[w * group + k] = sums[w * group + k] + weights[k] * landed
+            return tuple(sums)
+
+        sums = lax.fori_loop(
+            0, RELEASES, one_release, (jnp.zeros((depth, LANES), jnp.float32),) * (SCENARIOS * group), unroll=4
+        )
         for k in range(group):
             v = [sums[w * group + k] for w in range(SCENARIOS)]
             logs = jnp.log(v[0] * v[1] * (v[2] * v[3])) + jnp.log(v[4] * v[5] * (v[6] * v[7]))
@@ -501,7 +505,7 @@
                 pltpu.VMEM((scen_count, rows // 4, depth, LANES), f32),
                 pltpu.VMEM((scen_count, reach, depth, LANES), f32),
                 pltpu.VMEM((scen_count, reach // 4, depth, LANES), f32),
-                pltpu.VMEM((2 * reach * span, LANES), f32),
+                pltpu.VMEM((SHIFTS * reach * span, LANES), f32),
                 pltpu.VMEM((scen_count, rows, depth, LANES), f32),
                 pltpu.VMEM((scen_count, rows, depth, LANES), f32),
                 pltpu.VMEM((1, LANES), i32),
@@ -518,9 +522,6 @@
                 pltpu.SMEM(release_shifts.shape[::-1], i32),
                 pltpu.SMEM(price.shape, f32),
                 pltpu.SMEM((SCENARIOS * RELEASES,), i32),
-                pltpu.SMEM((SCENARIOS * RELEASES,), i32),
-                pltpu.SMEM((SCENARIOS * RELEASES,), i32),
-                pltpu.SMEM((SCENARIOS * RELEASES,), i32),
                 pltpu.SMEM((3 * RELEASES,), f32),
                 dma,
                 dma((3,)),
@@ -545,7 +546,7 @@
                 dma((far_count - 1,)),
             ],
             compiler_params=pltpu.CompilerParams(
-                collective_id=0, has_side_effects=True, vmem_limit_bytes=24 * 1024 * 1024
+                collective_id=0, has_side_effects=True, vmem_limit_bytes=52 * 1024 * 1024
             ),
         )(value_next, scenario_ids, inflow_table.T, release_shifts.T, price)
         return average - mean[0, 0]

time: 70.1 us -> 67 us (0.956)
  Pallas kernels: 66.7 us -> 63.4 us
    pallas_call x1, Pallas kernels: 66.7 us -> 63.4 us  [on_device(): pl.pallas_call(lambda *refs: kernel(dims, *refs), out_shape=(jax.ShapeDty...]
where the time goes in v5:
time: 67 us; the launch traced here: 66.7 us
  Pallas kernels  63.4 us (95%)
  local copies, waits for them, and re-layouts  1.7 us (3%)
  other arithmetic  0.87 us (1%)
  between operations  0.7 us (1%)
    pallas_call x1, Pallas kernels, on_device(): pl.pallas_call(lambda *refs: kernel(dims, *refs), out_shape=(jax.ShapeDty...  63.4 us
    unnamed x8, local copies, waits for them, and re-layouts  1.7 us

profile of v5, /device:TPU:1, one launch (start us, length us, event | category | flops | bytes accessed | tf_op | source)
XLA Modules:
  0.0 66.7 jit_solution(1262298226101627570)
XLA Ops:
  0.0 0.0 copy-start.2
  0.7 0.0 copy-start.1
  0.7 0.0 copy-start.3
  0.7 0.0 copy-done.2
  0.7 0.7 copy-done.1
  1.4 0.0 copy-done.3
  1.4 0.0 copy-start
  1.4 1.0 %copy-done = f32[16,8,1024]{2,1,0:T(8,128)S(1)} copy-done((f32[16,8,1024]{2,1,0:T(8,128)S(1)}, f32[16,8,1024]{2,1,0:T(8,128)}, u32[]{:S(2)}) %copy-start) | copy-done | bytes 524312
  2.4 63.4 %shard_map.55 = (f32[16,8,1024]{2,1,0:T(8,128)S(1)}, f32[1,128]{1,0:T(1,128)S(1)}) custom-call(f32[16,8,1024]{2,1,0:T(8,128)S(1)} %copy-done, s32[1]{0:T(128)S(6)} %copy.6.refs_1_, s32[3,12]{1,0:T(4,128)S(1)} %bitcast.4, s32[3,16]{1,0:T(4,128)S(1)} %bitcast.5, f32[3]{0:T(128)S(1)} %copy-done.3), custom_call_target="tpu_custom_call" | custom-call | tf_op jit(solution)/shard_map/pallas_call | solution.py:495
  65.8 0.9 %broadcast_subtract_fusion = f32[16,8,1024]{2,1,0:T(8,128)} fusion(f32[16,8,1024]{2,1,0:T(8,128)S(1)} %get-tuple-element.7, f32[]{:T(128)S(1)} %bitcast.6), kind=kLoop, calls=%fused_computation | loop fusion | flops 131072 | bytes 1048580 | tf_op jit(solution)/shard_map/sub | solution.py:552
Async XLA Ops:
  0.0 0.7 %copy-start.2 = (s32[16,3]{0,1:T(4,128)S(1)}, s32[16,3]{0,1:T(4,128)}, u32[]{:S(2)}) copy-start(s32[16,3]{0,1:T(4,128)} %param.8) | copy-start | bytes 580
  0.7 0.7 %copy-start.1 = (s32[12,3]{0,1:T(4,128)S(1)}, s32[12,3]{0,1:T(4,128)}, u32[]{:S(2)}) copy-start(s32[12,3]{0,1:T(4,128)} %param.7) | copy-start | bytes 436
  0.7 0.7 %copy-start.3 = (f32[3]{0:T(128)S(1)}, f32[3]{0:T(128)}, u32[]{:S(2)}) copy-start(f32[3]{0:T(128)} %refs_4_.1) | copy-start | bytes 40
  1.4 1.0 %copy-start = (f32[16,8,1024]{2,1,0:T(8,128)S(1)}, f32[16,8,1024]{2,1,0:T(8,128)}, u32[]{:S(2)}) copy-start(f32[16,8,1024]{2,1,0:T(8,128)} %refs_0_.1) | copy-start | bytes 1572868

commit v6 on v5

--- a/solution.py
+++ b/solution.py
@@ -404,7 +404,7 @@
             return tuple(sums)
 
         sums = lax.fori_loop(
-            0, RELEASES, one_release, (jnp.zeros((depth, LANES), jnp.float32),) * (SCENARIOS * group), unroll=4
+            0, RELEASES, one_release, (jnp.zeros((depth, LANES), jnp.float32),) * (SCENARIOS * group), unroll=8
         )
         for k in range(group):
             v = [sums[w * group + k] for w in range(SCENARIOS)]
@@ -546,7 +546,7 @@
                 dma((far_count - 1,)),
             ],
             compiler_params=pltpu.CompilerParams(
-                collective_id=0, has_side_effects=True, vmem_limit_bytes=52 * 1024 * 1024
+                collective_id=0, has_side_effects=True, vmem_limit_bytes=53 * 1024 * 1024
             ),
         )(value_next, scenario_ids, inflow_table.T, release_shifts.T, price)
         return average - mean[0, 0]

time: 67 us -> 65.4 us (0.976)
  local copies, waits for them, and re-layouts: 1.7 us -> 0.66 us
    unnamed x8 -> x6, local copies, waits for them, and re-layouts: 1.7 us -> 0.66 us
where the time goes in v6:
time: 65.4 us; the launch traced here: 65.3 us
  Pallas kernels  63.1 us (96%)
  other arithmetic  0.87 us (1%)
  between operations  0.7 us (1%)
  local copies, waits for them, and re-layouts  0.66 us (1%)
    pallas_call x1, Pallas kernels, on_device(): pl.pallas_call(lambda *refs: kernel(dims, *refs), out_shape=(jax.ShapeDty...  63.1 us

profile of v6, /device:TPU:1, one launch (start us, length us, event | category | flops | bytes accessed | tf_op | source)
XLA Modules:
  0.0 65.3 jit_solution(10763323495634680135)
XLA Ops:
  0.0 0.0 copy-start.1
  0.7 0.0 copy-start
  0.7 0.0 copy-start.2
  0.7 0.0 copy-done.1
  0.7 0.7 copy-done
  1.4 0.0 copy-done.2
  1.4 63.1 %shard_map.55 = (f32[16,8,1024]{2,1,0:T(8,128)S(1)}, f32[1,128]{1,0:T(1,128)S(1)}) custom-call(f32[16,8,1024]{2,1,0:T(8,128)} %refs_0_.1, s32[1]{0:T(128)S(6)} %copy.6.refs_1_, s32[3,12]{1,0:T(4,128)S(1)} %bitcast.4, s32[3,16]{1,0:T(4,128)S(1)} %bitcast.5, f32[3]{0:T(128)S(1)} %copy-done.2), custom_call_target="tpu_custom_call" | custom-call | tf_op jit(solution)/shard_map/pallas_call | solution.py:495
  64.4 0.9 %broadcast_subtract_fusion = f32[16,8,1024]{2,1,0:T(8,128)} fusion(f32[16,8,1024]{2,1,0:T(8,128)S(1)} %get-tuple-element.7, f32[]{:T(128)S(1)} %bitcast.6), kind=kLoop, calls=%fused_computation | loop fusion | flops 131072 | bytes 1048580 | tf_op jit(solution)/shard_map/sub | solution.py:552
Async XLA Ops:
  0.0 0.7 %copy-start.1 = (s32[16,3]{0,1:T(4,128)S(1)}, s32[16,3]{0,1:T(4,128)}, u32[]{:S(2)}) copy-start(s32[16,3]{0,1:T(4,128)} %param.8) | copy-start | bytes 580
  0.7 0.7 %copy-start = (s32[12,3]{0,1:T(4,128)S(1)}, s32[12,3]{0,1:T(4,128)}, u32[]{:S(2)}) copy-start(s32[12,3]{0,1:T(4,128)} %param.7) | copy-start | bytes 436
  0.7 0.7 %copy-start.2 = (f32[3]{0:T(128)S(1)}, f32[3]{0:T(128)}, u32[]{:S(2)}) copy-start(f32[3]{0:T(128)} %refs_4_.1) | copy-start | bytes 40
